TPU v7x, 32 devices: a whole 2x2x4 slice. The times are simulated.
32 devices in a mesh: grp: 2 (over x), tpl: 16 (over z, y, core).
Axes of the slice: x: 2, y: 2, z: 4, core: 2. Of those that a mesh axis runs over, the one named last changes fastest.
Arguments:
- strain_slots: bfloat16 [32, 3, 2, 262144], P(('grp', 'tpl')), parts along dimension 0, may hold values from -6 to 6
- templates: bfloat16 [32, 2, 262144], P(None, None, 'tpl'), may hold values from -6 to 6
- cutoffs: int32 [32], replicated, may hold values from 32768 to 262144
- lists: int32 [16, 2], replicated, may hold values from 0 to 31, as said below
- owner: int32 [2], P('grp'), parts along dimension 0, may hold values from 0 to 15
- slides: int32 [6], P('grp'), parts along dimension 0, may hold values from 0 to 262143
Outputs:
- peaks: float32 [64], P(('grp', 'tpl')), parts along dimension 0
- norms: float32 [64], P(('grp', 'tpl')), parts along dimension 0
There are 2 independent parts, one for each index of `grp`. A program takes and returns all parts, laid end to end along the dimension named above; an argument that names none is the same for every part. Nothing has to cross between parts.
Inputs may be any that keep to these rules, and one draw needn't show every extreme that they name: Every template appears once in lists; list positions in row-major order run through the templates by falling cutoffs. One template has cutoff 262144, one has 32768.
All inputs are finite; a program needn't handle non-finite values.
Results may differ from a plain program's by a relative error of at most 0.0021.
Values may be sent and summed in bfloat16 or wider, within the bound.
A program may use at most 128 MiB of HBM per device.

v0:
```python
import functools

import jax
import jax.numpy as jnp
import numpy as np
from jax import lax
from jax.experimental import pallas as pl
from jax.experimental.pallas import tpu as pltpu
from jax.sharding import PartitionSpec as P

ROWS = 512
COLS = 512
RADIX = 4
FOLD = ROWS // RADIX
WIDE = RADIX * COLS
HALF = COLS // 2

two_pi = 6.283185307179586
eps_norm = 1e-06


def turn_table(left_ids, right_ids, period):
    product_idx = left_ids[:, None] * right_ids[None, :] % period
    angles = product_idx.astype(np.float32) * np.float32(two_pi / period)
    return np.cos(angles), np.sin(angles)


def constant_tables():
    ids = np.arange(ROWS, dtype=np.int32)
    cos, sin = turn_table(ids[:FOLD], ids, ROWS)
    first = []
    for r in range(RADIX):
        c, s = cos[:, r::RADIX], sin[:, r::RADIX]
        first.append(np.concatenate([np.concatenate([c, -s], 1), np.concatenate([s, c], 1)], 0))
    twiddle = np.stack(turn_table(ids, ids, ROWS * COLS))
    cos, sin = turn_table(ids, ids[: HALF + 1], COLS)
    sin = sin[:, :HALF].copy()
    sin[:, 0] = cos[:, HALF]
    second = np.concatenate([cos[:, :HALF], sin], 1)
    return np.stack(first).astype(jnp.bfloat16), twiddle, second.astype(jnp.bfloat16)


def filter_kernel(
    cutoffs, strain, wave, row_phase, col_phase, first, twiddle, second,
    peaks, norms, turned, masked, twisted, total_q, total_r,
):
    dets = strain.shape[0]
    templates = wave.shape[0]
    bins = ROWS * COLS

    def turn(i, _):
        d, rows = i // 8, pl.ds(pl.multiple_of(i % 8 * 16, 16), 16)
        for c in range(WIDE // 512):
            cols = pl.ds(c * 512, 512)
            rr = jnp.concatenate([row_phase[d, 0, rows, :]] * 4, 1)
            ri = jnp.concatenate([row_phase[d, 1, rows, :]] * 4, 1)
            cr, ci = col_phase[d, 0, :, cols], col_phase[d, 1, :, cols]
            pr, pi = rr * cr - ri * ci, rr * ci + ri * cr
            xr = strain[d, 0, rows, cols].astype(jnp.float32)
            xi = strain[d, 1, rows, cols].astype(jnp.float32)
            turned[d, 0, rows, cols] = xr * pr - xi * pi
            turned[d, 1, rows, cols] = xr * pi + xi * pr
        return 0

    lax.fori_loop(0, dets * 8, turn, 0)

    def one_template(t, _):
        cutoff = cutoffs[t]

        blocks = 8 // wave.shape[3]

        def mask(i, acc):
            rows = pl.ds(pl.multiple_of(i * 8, 8), 8)
            for c in range(WIDE // 512):
                cols = pl.ds(c * 512, 512)
                at = (
                    lax.broadcasted_iota(jnp.int32, (8, 512), 0) + i * 8
                ) * WIDE + lax.broadcasted_iota(jnp.int32, (8, 512), 1) + c * 512
                inside = at < cutoff
                parts = []
                for p in range(2):
                    got = [
                        wave[t, p, i * blocks + e, :, cols].astype(jnp.float32) for e in range(blocks)
                    ]
                    got = got[0] if blocks == 1 else jnp.concatenate(got, 0)
                    parts.append(jnp.where(inside, got, 0.0))
                    masked[p, rows, cols] = parts[p]
                acc = acc + (parts[0] * parts[0] + parts[1] * parts[1])
            return acc

        acc = lax.fori_loop(0, FOLD // 8, mask, jnp.zeros((8, 512), jnp.float32))
        sigmasq = jnp.sum(acc)

        def one_detector(d, _):
            for c in range(COLS // 256):
                parts = []
                for r in range(RADIX):
                    cols = pl.ds(r * COLS + c * 256, 256)
                    xr, xi = turned[d, 0, :, cols], turned[d, 1, :, cols]
                    wr, wi = masked[0, :, cols], masked[1, :, cols]
                    product = jnp.concatenate([xr * wr + xi * wi, xi * wr - xr * wi], 0)
                    out = jnp.dot(
                        first[r], product.astype(jnp.bfloat16), preferred_element_type=jnp.float32
                    )
                    parts.append((out[:FOLD], out[FOLD:]))
                (r0, i0), (r1, i1), (r2, i2), (r3, i3) = parts
                ar, ai, br, bi = r0 + r2, i0 + i2, r0 - r2, i0 - i2
                cr, ci, dr, di = r1 + r3, i1 + i3, i3 - i1, r1 - r3
                sections = (
                    (ar + cr, ai + ci), (br + dr, bi + di), (ar - cr, ai - ci), (br - dr, bi - di)
                )
                cols = pl.ds(c * 256, 256)
                for q, (sr, si) in enumerate(sections):
                    rows = pl.ds(q * FOLD, FOLD)
                    tc, ts = twiddle[0, rows, cols], twiddle[1, rows, cols]
                    twisted[0, rows, cols] = (sr * tc - si * ts).astype(jnp.bfloat16)
                    twisted[1, rows, cols] = (sr * ts + si * tc).astype(jnp.bfloat16)
            for q in range(RADIX):
                rows = pl.ds(q * FOLD, FOLD)
                ac = jnp.dot(twisted[0, rows, :], second[...], preferred_element_type=jnp.float32)
                db = jnp.dot(twisted[1, rows, :], second[...], preferred_element_type=jnp.float32)
                a, c, dd, b = ac[:, :HALF], ac[:, HALF:], db[:, :HALF], db[:, HALF:]
                ad, bc = a * a + dd * dd, b * b + c * c
                both = ad + bc
                cross = 2.0 * (c * dd - a * b)
                lane = lax.broadcasted_iota(jnp.int32, both.shape, 1)
                edge = lane == 0
                both, cross = jnp.where(edge, 0.5 * both, both), jnp.where(edge, 0.5 * (ad - bc), cross)

                @pl.when(d == 0)
                def _():
                    total_q[rows, :] = both
                    total_r[rows, :] = cross

                @pl.when(d > 0)
                def _():
                    total_q[rows, :] += both
                    total_r[rows, :] += cross
            return 0

        lax.fori_loop(0, dets, one_detector, 0)

        def largest(i, acc):
            rows = pl.ds(pl.multiple_of(i * 32, 32), 32)
            return jnp.maximum(acc, total_q[rows, :] + jnp.abs(total_r[rows, :]))

        best = lax.fori_loop(0, ROWS // 32, largest, jnp.zeros((32, HALF), jnp.float32))
        peaks[t] = jnp.max(best) / (2.0 * (sigmasq + eps_norm))
        norms[t] = sigmasq / bins
        return 0

    lax.fori_loop(0, templates, one_template, 0)


def run_filter(cutoffs, strain, wave, row_phase, col_phase):
    templates, dets = wave.shape[0], strain.shape[0]
    first, twiddle, second = constant_tables()
    vmem = pl.BlockSpec(memory_space=pltpu.VMEM)
    smem = pl.BlockSpec(memory_space=pltpu.SMEM)
    out = jax.ShapeDtypeStruct((templates,), jnp.float32)
    return pl.pallas_call(
        filter_kernel,
        out_shape=(out, out),
        in_specs=[smem] + [vmem] * 7,
        out_specs=(smem, smem),
        scratch_shapes=[
            pltpu.VMEM((dets, 2, FOLD, WIDE), jnp.float32),
            pltpu.VMEM((2, FOLD, WIDE), jnp.float32),
            pltpu.VMEM((2, ROWS, COLS), jnp.bfloat16),
            pltpu.VMEM((ROWS, HALF), jnp.float32),
            pltpu.VMEM((ROWS, HALF), jnp.float32),
        ],
        compiler_params=pltpu.CompilerParams(vmem_limit_bytes=30 * 1024 * 1024),
        name="filter",
    )(cutoffs, strain, wave, row_phase, col_phase, jnp.asarray(first), jnp.asarray(twiddle), jnp.asarray(second))


def phases(slides):
    total = ROWS * COLS
    slides = slides[:, None]
    row = jnp.arange(FOLD, dtype=jnp.int32)[None] * slides % FOLD
    col = jnp.arange(WIDE, dtype=jnp.int32)[None] * slides % total
    row = row.astype(jnp.float32) * (two_pi / FOLD)
    col = col.astype(jnp.float32) * (two_pi / total)
    row = jnp.stack([jnp.cos(row), jnp.sin(row)], 1)
    col = jnp.stack([jnp.cos(col), jnp.sin(col)], 1)
    return jnp.broadcast_to(row[..., None], row.shape + (128,)), col[:, :, None, :]


MESH = pl.DeviceIdType.MESH


def share_kernel(
    width_y, flags, chosen, strain, bank, full, arrived, picked, other, ring_in, first_out,
    core_send, core_recv, sum_send, sum_recv, all_send, all_recv, part_send, part_recv,
    swap_send, swap_recv, own_sem, cross_send, cross_recv,
):
    n, groups = lax.axis_size("tpl"), lax.axis_size("grp")
    me, group = lax.axis_index("tpl"), lax.axis_index("grp")
    chips = n // 2
    core, chip = me % 2, me // 2
    depth = chips // width_y
    y, z = chip % width_y, chip // width_y
    pos = z + y * (2 * depth - 1 - 2 * z)
    half = strain.shape[1] // 2
    prow, pcol = ring_in.shape[3], ring_in.shape[4]
    colparts = strain.shape[2] // pcol
    subs = strain.shape[0]
    arm = chips // 2
    share = arrived.shape[0] // groups
    mine = pl.ds(group * share, share)
    partner = me + 1 - 2 * core

    def device_at(p):
        p = (p + chips) % chips
        yy = p // depth
        zz = p + yy * (2 * depth - 1 - 2 * p)
        return (zz * width_y + yy) * 2 + core

    nexts = (device_at(pos + 1), device_at(pos - 1))

    def chunk(direction, back):
        return (pos - back + 2 * chips) % chips if direction == 0 else (pos + back) % chips

    def spot(base, j):
        rows = pl.multiple_of(base + j // colparts * prow, prow)
        return pl.ds(rows, prow), pl.ds(pl.multiple_of(j % colparts * pcol, pcol), pcol)

    def piece(ref, base, direction, k, j):
        return ref.at[(k,) + spot(base, j)]

    def remote(src, dst, send, recv, **where):
        return pltpu.make_async_remote_copy(
            src_ref=src, dst_ref=dst, send_sem=send, recv_sem=recv,
            device_id=where, device_id_type=MESH,
        )

    def core_copy(back):
        j = chunk(0, back)
        planes = pl.ds(0, subs)
        return remote(
            strain.at[(planes,) + spot((1 - core) * half, j)],
            other.at[(planes,) + spot(0, j)],
            core_send.at[back], core_recv.at[back], tpl=partner,
        )

    def covered(direction, k):
        return (k < subs // 2) == (direction == 0)

    def sum_copy(direction, k, s, started=False):
        src = first_out.at[direction, k] if started else ring_in.at[max(s - 1, 0), direction, k]
        return remote(
            src, ring_in.at[s, direction, k],
            sum_send.at[s, direction, k], sum_recv.at[s, direction, k], tpl=nexts[direction],
        )

    def all_copy(direction, k, s):
        at = piece(full, core * half, direction, k, chunk(direction, s))
        return remote(
            at, at, all_send.at[s, direction, k], all_recv.at[s, direction, k], tpl=nexts[direction]
        )

    def part_copy(direction, k, s, base):
        at = piece(full, base, direction, k, chunk(direction, s))
        return remote(
            at, at, part_send.at[s, direction, k], part_recv.at[s, direction, k], tpl=partner
        )

    def swap_copy(i):
        to = (me - i + n) % n
        return remote(
            picked.at[to, mine], arrived.at[mine, me], swap_send.at[i], swap_recv.at[i], tpl=to
        )

    def swap_arrival(i):
        source = (me + i) % n
        return remote(
            picked.at[me, mine], arrived.at[mine, source], swap_send.at[i], swap_recv.at[i], tpl=source
        )

    def cross_copy(i, g):
        at = arrived.at[mine, (me + i) % n]
        return remote(
            at, at, cross_send.at[g - 1, i], cross_recv.at[g - 1, i], grp=(group + g) % groups
        )

    def cross_arrival(i, g):
        source = (group - g + groups) % groups
        at = arrived.at[pl.ds(source * share, share), (me + i) % n]
        return remote(at, at, cross_send.at[g - 1, i], cross_recv.at[g - 1, i], grp=source)

    barrier = pltpu.get_barrier_semaphore()

    def greet(i, _):
        pl.semaphore_signal(barrier, inc=1, device_id={"tpl": (me + i) % n}, device_id_type=MESH)
        return 0

    lax.fori_loop(1, n, greet, 0)
    for g in range(1, groups):
        pl.semaphore_signal(
            barrier, inc=1, device_id={"grp": (group + g) % groups}, device_id_type=MESH
        )
    pl.semaphore_wait(barrier, n - 1 + groups - 1)

    order = [arm]
    for h in range(arm - 1, 0, -1):
        order += [h, chips - h]
    order.append(0)
    for back in order:
        core_copy(back).start()
    i_own, chip_owns, from_left = flags[0], flags[1], flags[2]
    slots = picked.shape[1] // 2

    def gather(i, _):
        for e in range(slots):
            picked[i, pl.ds(2 * e, 2)] = bank[chosen[i * slots + e]]
        return 0

    lax.fori_loop(0, n, gather, 0)
    own = pltpu.make_async_copy(picked.at[me], arrived.at[:, me], own_sem)
    own.start()
    per_step = -(-(n - 1) // (arm - 1))
    late_step = -(-(n - 1) // (2 * arm - 3))

    def cross_start(i):
        swap_arrival(i).wait_recv()
        for g in range(1, groups):
            cross_copy(i, g).start()

    def templates_on(step):
        for at in range(1 + step * per_step, min(n, 1 + (step + 1) * per_step)):
            swap_copy(at).start()
        late = 1 + (step - 2) * late_step
        for at in range(max(late, 1), min(n, late + late_step)):
            cross_start(at)

    def candidate(direction, k, j):
        here = piece(strain, core * half, direction, k, j)[...]
        there = piece(other, 0, direction, k, j)[...]
        return jnp.where(i_own != 0, here, there)

    core_copy(arm).wait_recv()
    for k in range(subs):
        direction = 0 if covered(0, k) else 1
        first_out[direction, k] = candidate(direction, k, chunk(1, arm))
        sum_copy(direction, k, 0, True).start()
    for back in (arm - 1, chips - arm + 1):
        core_copy(back).wait_recv()
    for k in range(subs):
        direction = 1 if covered(0, k) else 0
        first_out[direction, k] = candidate(direction, k, chunk(1 - direction, arm - 1))
        sum_copy(direction, k, 1, True).start()
    for s in range(arm - 1):
        h = arm - 1 - s
        if s > 0:
            for back in (h, chips - h):
                core_copy(back).wait_recv()
        for k in range(subs):
            for direction in range(2):
                if s > 0 or covered(direction, k):
                    sum_copy(direction, k, s).wait_recv()
                    ring_in[s, direction, k] = jnp.where(
                        chip_owns != 0,
                        candidate(direction, k, chunk(1 - direction, h)),
                        ring_in[s, direction, k],
                    )
                    sum_copy(direction, k, s + 1).start()
        templates_on(s)
    core_copy(0).wait_recv()
    for k in range(subs):
        for direction in range(2):
            sum_copy(direction, k, arm - 1).wait_recv()
        left = from_left + (flags[3] if covered(0, k) else 0)
        best = jnp.where(left != 0, ring_in[arm - 1, 0, k], ring_in[arm - 1, 1, k])
        piece(full, core * half, 0, k, pos)[...] = jnp.where(
            chip_owns != 0, candidate(0, k, pos), best
        )
        for direction in range(2):
            all_copy(direction, k, 0).start()
        part_copy(0, k, 0, core * half).start()
    for s in range(arm):
        for k in range(subs):
            for direction in range(2):
                if s < arm - 1 or covered(direction, k):
                    at = piece(full, core * half, direction, k, chunk(direction, s + 1))
                    remote(
                        at, at, all_send.at[s, direction, k], all_recv.at[s, direction, k],
                        tpl=nexts[direction],
                    ).wait_recv()
                    if s + 1 < arm - 1 or (s + 1 == arm - 1 and covered(direction, k)):
                        all_copy(direction, k, s + 1).start()
                    part_copy(direction, k, s + 1, core * half).start()
        templates_on(arm - 1 + s)
    for back in range(chips):
        core_copy(back).wait_send()
    for s in range(arm + 1):
        for k in range(subs):
            for direction in range(2):
                if (s == 0 and direction == 0) or 0 < s < arm or (s == arm and covered(direction, k)):
                    part_copy(direction, k, s, core * half).wait_send()
                    part_copy(direction, k, s, (1 - core) * half).wait_recv()
                if s < arm - 1 or (s == arm - 1 and covered(direction, k)):
                    all_copy(direction, k, s).wait_send()
                if 0 < s < arm or (s == 0 and covered(direction, k)):
                    sum_copy(direction, k, s).wait_send()

    def finish_swap(i, _):
        swap_copy(i).wait_send()
        for g in range(1, groups):
            cross_copy(i, g).wait_send()
            cross_arrival(i, g).wait_recv()
        return 0

    lax.fori_loop(1, n, finish_swap, 0)
    own.wait()


def run_share(width_y, flags, chosen, strain, bank):
    n, groups = lax.axis_size("tpl"), lax.axis_size("grp")
    chips = n // 2
    planes, high, wide = strain.shape
    subs = planes
    rowparts = max(1, chips * 256 // wide)
    prow, pcol = high // 2 // rowparts, wide * rowparts // chips
    vmem = pl.BlockSpec(memory_space=pltpu.VMEM)
    dma = pltpu.SemaphoreType.DMA
    pieces = chosen.shape[0] // n * 2
    arrived = (pieces, n) + bank.shape[2:]
    return pl.pallas_call(
        functools.partial(share_kernel, width_y),
        out_shape=(
            jax.ShapeDtypeStruct(strain.shape, strain.dtype),
            jax.ShapeDtypeStruct(arrived, bank.dtype),
        ),
        in_specs=[pl.BlockSpec(memory_space=pltpu.SMEM)] * 2 + [vmem, vmem],
        out_specs=(vmem, vmem),
        scratch_shapes=[
            pltpu.VMEM((n, pieces) + bank.shape[2:], bank.dtype),
            pltpu.VMEM((planes, high // 2, wide), strain.dtype),
            pltpu.VMEM((chips // 2, 2, subs, prow, pcol), strain.dtype),
            pltpu.VMEM((2, subs, prow, pcol), strain.dtype),
            dma((chips,)), dma((chips,)),
            dma((chips // 2, 2, subs)), dma((chips // 2, 2, subs)),
            dma((chips // 2, 2, subs)), dma((chips // 2, 2, subs)),
            dma((chips // 2 + 1, 2, subs)), dma((chips // 2 + 1, 2, subs)),
            dma((n,)), dma((n,)), dma,
            dma((max(1, groups - 1), n)), dma((max(1, groups - 1), n)),
        ],
        compiler_params=pltpu.CompilerParams(
            collective_id=0, has_side_effects=True, vmem_limit_bytes=22 * 1024 * 1024
        ),
        name="share",
    )(flags, chosen, strain, bank)


def body(width_y, strain_slots, templates, cutoffs, lists, owner, slides):
    devices = lax.axis_size("tpl")
    own_index = lax.axis_index("tpl")
    per_device = lists.shape[1]
    chosen = lists.reshape(-1)
    dets = strain_slots.shape[1]
    strain = strain_slots[0].reshape(dets * 2, FOLD, WIDE)
    chips = devices // 2
    depth = chips // width_y

    def place(device):
        chip = device // 2
        return chip // width_y + chip % width_y * (2 * depth - 1 - 2 * (chip // width_y))

    ahead = (place(owner[0]) - place(own_index)) % chips
    flags = jnp.stack([own_index == owner[0], ahead == 0, ahead > chips // 2, ahead == chips // 2])
    flags = flags.astype(jnp.int32)
    rows = templates.shape[2] // WIDE
    bank = templates.reshape(-1, 2, rows, WIDE)
    strain, arrived = run_share(width_y, flags, chosen, strain, bank)
    strain = strain.reshape(dets, 2, FOLD, WIDE)
    arrived = arrived.reshape(per_device, 2, devices, rows, WIDE)
    own_ids = lax.dynamic_index_in_dim(lists, own_index, 0, keepdims=False)
    row_phase, col_phase = phases(slides)
    return run_filter(cutoffs[own_ids], strain, arrived, row_phase, col_phase)


def solution(mesh):
    in_specs = (
        P(("grp", "tpl"), None, None, None),
        P(None, None, "tpl"),
        P(),
        P(),
        P("grp"),
        P("grp"),
    )
    out_specs = (P(("grp", "tpl")), P(("grp", "tpl")))
    width_y = len({d.coords[1] for d in mesh.devices[0].flat})
    return jax.shard_map(functools.partial(body, width_y), mesh=mesh, in_specs=in_specs, out_specs=out_specs, check_vma=False)
```

profile of v0, /device:TPU:0, one launch (start us, length us, event | category | flops | bytes accessed | tf_op | source)
XLA Modules:
  0.0 107.6 jit_solution(14488757607101674445)
XLA Ops:
  0.6 0.0 copy-start
  0.6 0.9 dynamic-slice_reduce_fusion
  1.5 0.0 copy-done
  1.5 0.6 gather_fusion
  2.9 0.1 add_convert_fusion.flags
  3.0 0.8 copy.12
  3.8 0.1 reshape.225.chosen
  3.9 4.5 %reshape_squeeze.3.strain = bf16[6,128,2048]{2,1,0:T(8,128)(2,1)S(1)} reshape(bf16[1,3,2,262144]{3,2,1,0:T(2,128)(2,1)} %param.9) | data formatting | bytes 6291456 | tf_op jit(solution)/shard_map/reshape;squeeze | solution.py:462
  8.4 4.5 %reshape.226.bank = bf16[32,2,8,2048]{3,2,1,0:T(8,128)(2,1)} reshape(bf16[32,2,16384]{2,1,0:T(2,128)(2,1)} %param.10) | data formatting | bytes 4194304 | tf_op jit(solution)/shard_map/reshape | solution.py:474
  12.9 0.0 copy-start.1
  12.9 1.6 %copy-done.1 = bf16[32,2,8,2048]{3,2,1,0:T(8,128)(2,1)S(1)} copy-done((bf16[32,2,8,2048]{3,2,1,0:T(8,128)(2,1)S(1)}, bf16[32,2,8,2048]{3,2,1,0:T(8,128)(2,1)}, u32[]{:S(2)}) %copy-start.1) | copy-done | bytes 2097176
  14.5 0.0 copy-start.5
  14.5 0.0 copy-start.2
  14.5 0.0 copy-start.3
  14.5 0.0 copy-start.4
  14.5 72.1 %share.1 = (bf16[6,128,2048]{2,1,0:T(8,128)(2,1)S(1)}, bf16[4,16,8,2048]{3,2,1,0:T(8,128)(2,1)S(1)}) custom-call(s32[4]{0:T(128)S(1)} %add_convert_fusion.flags, s32[32]{0:T(128)S(1)} %reshape.225.chosen, bf16[6,128,2048]{2,1,0:T(8,128)(2,1)S(1)} %reshape_squeeze.3.strain, bf16[32,2,8,2048]{3,2,1,0:T(8,128)(2,1)S(1)} %copy-done.1), custom_call_target="tpu_custom_call" | custom-call | tf_op jit(solution)/shard_map/share/pallas_call | solution.py:429
  86.6 0.0 copy-done.5
  86.6 0.1 fusion.9
  86.8 0.2 broadcast_in_dim.4.row_phase
  86.9 0.8 fusion.4
  87.8 0.1 pad_maximum_fusion
  87.9 0.0 copy-done.2
  87.9 0.0 copy-done.3
  87.9 0.0 copy-done.4
  87.9 19.7 %filter.1 = (f32[2]{0:T(128)}, f32[2]{0:T(128)}) custom-call(s32[2]{0:T(128)S(1)} %gather_fusion, bf16[3,2,128,2048]{3,2,1,0:T(8,128)(2,1)S(1)} %bitcast.16, bf16[2,2,16,8,2048]{4,3,2,1,0:T(8,128)(2,1)S(1)} %bitcast.17, f32[3,2,128,128]{3,2,1,0:T(8,128)S(1)} %broadcast_in_dim.4.row_phase, f32[3,2,1,2048]{3,2,1,0:T(1,128)S(1)} %broadcast_in_dim.5.col_phase, ...), custom_call_target="tpu_custom_call" | custom-call | tf_op jit(solution)/shard_map/filter/pallas_call | solution.py:161
  (4 shorter events, 0.1 us)
Async XLA Ops:
  0.6 0.9 copy-start
  12.9 1.6 %copy-start.1 = (bf16[32,2,8,2048]{3,2,1,0:T(8,128)(2,1)S(1)}, bf16[32,2,8,2048]{3,2,1,0:T(8,128)(2,1)}, u32[]{:S(2)}) copy-start(bf16[32,2,8,2048]{3,2,1,0:T(8,128)(2,1)} %reshape.226.bank) | copy-start | bytes 6291460
  14.5 72.2 %copy-start.5 = (s32[3]{0:T(128)S(1)}, s32[3]{0:T(128)}, u32[]{:S(2)}) copy-start(s32[3]{0:T(128)} %param.14) | copy-start | bytes 40
  14.5 73.4 %copy-start.2 = (f32[2,512,512]{2,1,0:T(8,128)S(1)}, f32[2,512,512]{2,1,0:T(8,128)}, u32[]{:S(2)}) copy-start(f32[2,512,512]{2,1,0:T(8,128)} %constant.118.clone.twiddle) | copy-start | bytes 6291460
  14.5 73.5 %copy-start.3 = (bf16[4,256,256]{2,1,0:T(8,128)(2,1)S(1)}, bf16[4,256,256]{2,1,0:T(8,128)(2,1)}, u32[]{:S(2)}) copy-start(bf16[4,256,256]{2,1,0:T(8,128)(2,1)} %constant.117.clone.first) | copy-start | bytes 1572868
  14.5 73.5 %copy-start.4 = (bf16[512,512]{1,0:T(8,128)(2,1)S(1)}, bf16[512,512]{1,0:T(8,128)(2,1)}, u32[]{:S(2)}) copy-start(bf16[512,512]{1,0:T(8,128)(2,1)} %constant.119.clone.second) | copy-start | bytes 1572868
where the time goes:
time: 108 us
  Pallas kernels  91.8 us (85%)
  local copies, waits for them, and re-layouts  13.1 us (12%)
  between operations  1.52 us (1%)
  other arithmetic  1.13 us (1%)
    pallas_call x1, Pallas kernels, run_share(): pl.pallas_call(functools.partial(share_kernel, width_y), out_shape=(jax.S...  72.1 us
    pallas_call x1, Pallas kernels, run_filter(): pl.pallas_call(filter_kernel, out_shape=(out, out), in_specs=[smem] + [vm...  19.7 us
    another operation x1, local copies, waits for them, and re-layouts, body(): strain = strain_slots[0].reshape(dets * 2, FOLD, WIDE)  4.51 us
    reshape x1, local copies, waits for them, and re-layouts, body(): bank = templates.reshape(-1, 2, rows, WIDE)  4.47 us
    unnamed x13, local copies, waits for them, and re-layouts  2.37 us

commit v1 on v0

v1 whole, which is shorter than its diff:
```python
import functools

import jax
import jax.numpy as jnp
import numpy as np
from jax import lax
from jax.experimental import pallas as pl
from jax.experimental.pallas import tpu as pltpu
from jax.sharding import PartitionSpec as P

ROWS = 512
COLS = 512
RADIX = 4
FOLD = ROWS // RADIX
WIDE = RADIX * COLS
HALF = COLS // 2
LANES = 128
CHUNKS = WIDE // LANES
TALL = 2 * FOLD * CHUNKS

two_pi = 6.283185307179586
eps_norm = 1e-06

MESH = pl.DeviceIdType.MESH
LEAD = 2
LAG = 2
CROSS_LAG = 3


def turn_table(left_ids, right_ids, period):
    product_idx = left_ids[:, None] * right_ids[None, :] % period
    angles = product_idx.astype(np.float32) * np.float32(two_pi / period)
    return np.cos(angles), np.sin(angles)


def constant_tables():
    ids = np.arange(ROWS, dtype=np.int32)
    cos, sin = turn_table(ids[:FOLD], ids, ROWS)
    first = []
    for r in range(RADIX):
        c, s = cos[:, r::RADIX], sin[:, r::RADIX]
        first.append(np.concatenate([np.concatenate([c, -s], 1), np.concatenate([s, c], 1)], 0))
    twiddle = np.stack(turn_table(ids, ids, ROWS * COLS))
    cos, sin = turn_table(ids, ids[: HALF + 1], COLS)
    sin = sin[:, :HALF].copy()
    sin[:, 0] = cos[:, HALF]
    second = np.concatenate([cos[:, :HALF], sin], 1)
    return np.stack(first).astype(jnp.bfloat16), twiddle, second.astype(jnp.bfloat16)


def send_order(depth):
    orders = []
    for z in range(depth):
        need = [(depth - 1 - j + z if j > z else j + depth - 1 - z if j < z else depth, j) for j in range(depth)]
        orders.append([j for _, j in sorted(need)])
    return orders


def kernel(
    width, lists, owner, cutoffs, slides, strain, bank_hbm, first_hbm, twiddle_hbm, second_hbm,
    peaks, norms,
    mine, other, ysend, yrecv, zin, full, bank, picked, arrived, flat, row_phase, col_phase,
    turned, masked, twisted, total_q, total_r, first, twiddle, second,
    local_sem, core_send, core_recv, y_send, y_recv, z_send, z_recv, ag_send, ag_recv,
    yag_send, yag_recv, part_send, part_recv, swap_send, swap_recv, cross_send, cross_recv,
):
    n, groups = lax.axis_size("tpl"), lax.axis_size("grp")
    me, group = lax.axis_index("tpl"), lax.axis_index("grp")
    depth = n // 2 // width
    core, chip = me % 2, me // 2
    y, z = chip % width, chip // width
    dets = strain.shape[0]
    half = strain.shape[1] // 2
    prow = half // (width * depth)
    slots = lists.shape[0]
    shard = bank.shape[1]
    hrow = shard // groups
    partner = me + 1 - 2 * core

    def device(yy, zz):
        return (zz * width + yy) * 2 + core

    across = device(width - 1 - y, z)
    onward = (device(y, jnp.minimum(z + 1, depth - 1)), device(y, jnp.maximum(z - 1, 0)))

    own_id = owner[0]
    own_chip = own_id // 2
    i_own = own_id == me
    chip_owns = own_chip == chip
    line_owns = own_chip // width == z
    from_left = own_chip // width < z

    def remote(src, dst, send, recv, **where):
        return pltpu.make_async_remote_copy(
            src_ref=src, dst_ref=dst, send_sem=send, recv_sem=recv, device_id=where, device_id_type=MESH
        )

    def rows(base, size):
        return pl.ds(pl.multiple_of(base, 16), size)

    def place(yy, j):
        return rows((yy * depth + j) * prow, prow)

    def spot(cc, yy, j):
        return rows(cc * half + (yy * depth + j) * prow, prow)

    def core_copy(s, yy, j):
        k = yy * depth + j
        return remote(
            strain.at[s, spot(1 - core, yy, j)], other.at[s, place(yy, j)],
            core_send.at[s, k], core_recv.at[s, k], tpl=partner,
        )

    def y_copy(s, j):
        return remote(ysend.at[s, j], yrecv.at[s, j], y_send.at[s, j], y_recv.at[s, j], tpl=across)

    def z_copy(way, s, j):
        at = zin.at[way, s, j]
        return remote(at, at, z_send.at[way, s, j], z_recv.at[way, s, j], tpl=onward[way])

    def ag_copy(way, s, j):
        at = full.at[s, spot(core, y, j)]
        return remote(at, at, ag_send.at[way, s, j], ag_recv.at[way, s, j], tpl=onward[way])

    def yag_copy(s, j):
        at = full.at[s, spot(core, y, j)]
        return remote(at, at, yag_send.at[s, j], yag_recv.at[s, j], tpl=across)

    def part_copy(s, cc, yy, j):
        at = full.at[s, spot(cc, yy, j)]
        k = yy * depth + j
        return remote(at, at, part_send.at[s, k], part_recv.at[s, k], tpl=partner)

    def swap_copy(slot, i):
        to = (me - i + n) % n
        return remote(
            picked.at[slot, to], arrived.at[slot, me, rows(group * hrow, hrow)],
            swap_send.at[slot, i], swap_recv.at[slot, i], tpl=to,
        )

    def swap_arrival(slot, i):
        source = (me + i) % n
        return remote(
            picked.at[slot, me], arrived.at[slot, source, rows(group * hrow, hrow)],
            swap_send.at[slot, i], swap_recv.at[slot, i], tpl=source,
        )

    def cross_copy(slot, i, g):
        at = arrived.at[slot, (me + i) % n, rows(group * hrow, hrow)]
        return remote(
            at, at, cross_send.at[slot, g - 1, i], cross_recv.at[slot, g - 1, i], grp=(group + g) % groups
        )

    def cross_arrival(slot, i, g):
        source = (group - g + groups) % groups
        at = arrived.at[slot, (me + i) % n, rows(source * hrow, hrow)]
        return remote(at, at, cross_send.at[slot, g - 1, i], cross_recv.at[slot, g - 1, i], grp=source)

    locals_ = [
        pltpu.make_async_copy(strain.at[:, rows(core * half, half)], mine, local_sem.at[0]),
        pltpu.make_async_copy(bank_hbm, bank, local_sem.at[1]),
        pltpu.make_async_copy(first_hbm, first, local_sem.at[2]),
        pltpu.make_async_copy(twiddle_hbm, twiddle, local_sem.at[3]),
        pltpu.make_async_copy(second_hbm, second, local_sem.at[4]),
    ]
    for copy in locals_[:2]:
        copy.start()

    barrier = pltpu.get_barrier_semaphore()

    def greet(i, _):
        pl.semaphore_signal(barrier, inc=1, device_id={"tpl": (me + i) % n}, device_id_type=MESH)
        return 0

    lax.fori_loop(1, n, greet, 0)
    for g in range(1, groups):
        pl.semaphore_signal(barrier, inc=1, device_id={"grp": (group + g) % groups}, device_id_type=MESH)
    pl.semaphore_wait(barrier, n - 1 + groups - 1)

    orders = send_order(depth)

    def ordered(o):
        j = 0
        for zz in range(depth):
            j = jnp.where(z == zz, orders[zz][o], j)
        return j

    def start_core(s):
        for o in range(depth):
            for yy in (width - 1 - y, y)[2 - width:]:
                core_copy(s, yy, ordered(o)).start()

    def candidate(s, yy, j):
        return jnp.where(i_own, mine[s, place(yy, j)], other[s, place(yy, j)])

    def open_det(s):
        if width == 1:
            return
        for o in range(depth):
            j = ordered(o)
            core_copy(s, 1 - y, j).wait_recv()
            ysend[s, j] = candidate(s, 1 - y, j)
            y_copy(s, j).start()

    def merged(s, j):
        core_copy(s, y, j).wait_recv()
        got = candidate(s, y, j)
        if width == 1:
            return got
        y_copy(s, j).wait_recv()
        return jnp.where(chip_owns, got, yrecv[s, j])

    def pass_on(s, j):
        if width > 1:
            yag_copy(s, j).start()
        part_copy(s, core, y, j).start()

    def reduce_step(s, step):
        for way in range(2):
            behind = z if way == 0 else depth - 1 - z
            j = depth - 1 - step + z if way == 0 else step - (depth - 1 - z)

            @pl.when((step >= behind) & (step < depth - 1))
            def _():
                value = merged(s, j)

                @pl.when(behind == 0)
                def _():
                    zin[way, s, j] = value

                @pl.when(behind > 0)
                def _():
                    z_copy(way, s, j).wait_recv()
                    zin[way, s, j] = jnp.where(line_owns, value, zin[way, s, j])

                z_copy(way, s, j).start()

        @pl.when(step == depth - 1)
        def _():
            value = merged(s, z)

            @pl.when(z > 0)
            def _():
                z_copy(0, s, z).wait_recv()

            @pl.when(z < depth - 1)
            def _():
                z_copy(1, s, z).wait_recv()

            @pl.when(z == 0)
            def _():
                full[s, spot(core, y, z)] = jnp.where(line_owns, value, zin[1, s, z])

            @pl.when(z == depth - 1)
            def _():
                full[s, spot(core, y, z)] = jnp.where(line_owns, value, zin[0, s, z])

            @pl.when((z > 0) & (z < depth - 1))
            def _():
                full[s, spot(core, y, z)] = jnp.where(
                    line_owns, value, jnp.where(from_left, zin[0, s, z], zin[1, s, z])
                )

            @pl.when(z < depth - 1)
            def _():
                ag_copy(0, s, z).start()

            @pl.when(z > 0)
            def _():
                ag_copy(1, s, z).start()

            pass_on(s, z)

    def gather_step(s, h):
        for way in range(2):
            j = z - h if way == 0 else z + h
            ahead = depth - 1 - z if way == 0 else z

            @pl.when((h >= 1) & (h < depth) & (j >= 0) & (j < depth))
            def _():
                ag_copy(way, s, j).wait_recv()

                @pl.when(ahead > 0)
                def _():
                    ag_copy(way, s, j).start()

                pass_on(s, j)

    def hand_step(s, h):
        if width == 1:
            return
        for way in range(2):
            j = z - h if way == 0 else z + h

            @pl.when((h >= way) & (h < depth) & (j >= 0) & (j < depth))
            def _():
                at = full.at[s, spot(core, 1 - y, j)]
                remote(at, at, yag_send.at[s, j], yag_recv.at[s, j], tpl=across).wait_recv()
                part_copy(s, core, 1 - y, j).start()

    for s in range(dets):
        start_core(s)
    locals_[0].wait()
    open_det(0)
    for copy in locals_[2:]:
        copy.start()
    locals_[1].wait()

    def pick(d, _):
        for slot in range(slots):
            picked[slot, d] = bank[lists[slot, d], rows(group * hrow, hrow)]
        return 0

    lax.fori_loop(0, n, pick, 0)
    for slot in range(slots):
        arrived[slot, me] = bank[lists[slot, me]]

    steps = LEAD * (dets - 1) + 2 * (depth - 1) + LAG + 1
    messages = slots * (n - 1)
    per_step = -(-messages // (steps - CROSS_LAG))

    def swap_start(q):
        swap_copy(q // (n - 1), 1 + q % (n - 1)).start()

    def cross_start(q):
        slot, i = q // (n - 1), 1 + q % (n - 1)
        swap_arrival(slot, i).wait_recv()
        for g in range(1, groups):
            cross_copy(slot, i, g).start()

    def step_body(t, _):
        for s in range(dets):
            if s > 0:
                @pl.when(t == LEAD * s - 1)
                def _():
                    open_det(s)
            reduce_step(s, t - LEAD * s)
            gather_step(s, t - LEAD * s - (depth - 1))
            hand_step(s, t - LEAD * s - (depth - 1) - LAG)
        for e in range(per_step):
            q = t * per_step + e

            @pl.when(q < messages)
            def _():
                swap_start(q)

            p = (t - CROSS_LAG) * per_step + e

            @pl.when((p >= 0) & (p < messages))
            def _():
                cross_start(p)
        return 0

    lax.fori_loop(0, steps, step_body, 0)

    def drain(j, _):
        for s in range(dets):
            for yy in range(width):
                core_copy(s, yy, j).wait_send()
                part_copy(s, core, yy, j).wait_send()
                part_copy(s, 1 - core, yy, j).wait_recv()
            if width > 1:
                y_copy(s, j).wait_send()
                yag_copy(s, j).wait_send()
            for way in range(2):
                ahead = depth - 1 - z if way == 0 else z
                passes = j > z if way == 0 else j < z

                @pl.when((ahead > 0) & passes)
                def _():
                    z_copy(way, s, j).wait_send()

                @pl.when((ahead > 0) & jnp.logical_not(passes))
                def _():
                    ag_copy(way, s, j).wait_send()
        return 0

    lax.fori_loop(0, depth, drain, 0)

    def finish_swap(i, _):
        for slot in range(slots):
            swap_copy(slot, i).wait_send()
            for g in range(1, groups):
                cross_copy(slot, i, g).wait_send()
                cross_arrival(slot, i, g).wait_recv()
        return 0

    lax.fori_loop(1, n, finish_swap, 0)
    for copy in locals_[2:]:
        copy.wait()

    make_phases(slides, row_phase, col_phase)
    for d in range(dets):
        turn_det(full.at[d], flat, row_phase.at[d], col_phase.at[d], turned.at[d])
    for slot in range(slots):
        cutoff = cutoffs[lists[slot, me]]
        sigmasq = mask_template(cutoff, arrived.at[slot], flat, masked)
        peak = filter_template(turned, masked, first, twiddle, second, twisted, total_q, total_r)
        peaks[slot] = peak / (2.0 * (sigmasq + eps_norm))
        norms[slot] = sigmasq / (ROWS * COLS)


def make_phases(slides, row_phase, col_phase):
    total = ROWS * COLS
    for d in range(row_phase.shape[0]):
        slide = slides[d]
        row = lax.broadcasted_iota(jnp.int32, (FOLD, LANES), 0) * slide % FOLD
        row = row.astype(jnp.float32) * (two_pi / FOLD)
        row_phase[d, 0] = jnp.cos(row)
        row_phase[d, 1] = jnp.sin(row)
        col = lax.broadcasted_iota(jnp.int32, (8, WIDE), 1) * slide % total
        col = col.astype(jnp.float32) * (two_pi / total)
        col_phase[d, 0] = jnp.cos(col)
        col_phase[d, 1] = jnp.sin(col)


def widen(source, flat):
    size = 256

    def body(i, _):
        at = pl.ds(pl.multiple_of(i * size, size), size)
        flat[at, :] = source[at, :].astype(jnp.float32)
        return 0

    lax.fori_loop(0, TALL // size, body, 0)


def tile(flat, i, c, part):
    return flat[pl.ds((i * 8 * CHUNKS + c) * 2 + part, 8, stride=2 * CHUNKS), :]


def turn_det(source, flat, row_phase, col_phase, turned):
    widen(source, flat)

    def body(i, _):
        at = pl.ds(pl.multiple_of(i * 8, 8), 8)
        rr, ri = row_phase[0, at, :], row_phase[1, at, :]
        for c in range(CHUNKS):
            cols = pl.ds(c * LANES, LANES)
            cr, ci = col_phase[0, :, cols], col_phase[1, :, cols]
            pr, pi = rr * cr - ri * ci, rr * ci + ri * cr
            xr, xi = tile(flat, i, c, 0), tile(flat, i, c, 1)
            turned[0, at, cols] = xr * pr - xi * pi
            turned[1, at, cols] = xr * pi + xi * pr
        return 0

    lax.fori_loop(0, FOLD // 8, body, 0)


def mask_template(cutoff, source, flat, masked):
    shards, shard = source.shape[0], source.shape[1]

    def body(i, _):
        flat[pl.ds(pl.multiple_of(i * shard, shard), shard), :] = source[i].astype(jnp.float32)
        return 0

    lax.fori_loop(0, shards, body, 0)

    def mask(i, acc):
        at = pl.ds(pl.multiple_of(i * 8, 8), 8)
        base = (lax.broadcasted_iota(jnp.int32, (8, LANES), 0) + i * 8) * WIDE + lax.broadcasted_iota(
            jnp.int32, (8, LANES), 1
        )
        for c in range(CHUNKS):
            cols = pl.ds(c * LANES, LANES)
            inside = base < cutoff - c * LANES
            wr = jnp.where(inside, tile(flat, i, c, 0), 0.0)
            wi = jnp.where(inside, tile(flat, i, c, 1), 0.0)
            masked[0, at, cols] = wr
            masked[1, at, cols] = wi
            acc = acc + (wr * wr + wi * wi)
        return acc

    return jnp.sum(lax.fori_loop(0, FOLD // 8, mask, jnp.zeros((8, LANES), jnp.float32)))


def filter_template(turned, masked, first, twiddle, second, twisted, total_q, total_r):
    dets = turned.shape[0]

    def one_detector(d, _):
        for c in range(COLS // 256):
            parts = []
            for r in range(RADIX):
                cols = pl.ds(r * COLS + c * 256, 256)
                xr, xi = turned[d, 0, :, cols], turned[d, 1, :, cols]
                wr, wi = masked[0, :, cols], masked[1, :, cols]
                product = jnp.concatenate([xr * wr + xi * wi, xi * wr - xr * wi], 0)
                out = jnp.dot(first[r], product.astype(jnp.bfloat16), preferred_element_type=jnp.float32)
                parts.append((out[:FOLD], out[FOLD:]))
            (r0, i0), (r1, i1), (r2, i2), (r3, i3) = parts
            ar, ai, br, bi = r0 + r2, i0 + i2, r0 - r2, i0 - i2
            cr, ci, dr, di = r1 + r3, i1 + i3, i3 - i1, r1 - r3
            sections = (
                (ar + cr, ai + ci), (br + dr, bi + di), (ar - cr, ai - ci), (br - dr, bi - di)
            )
            cols = pl.ds(c * 256, 256)
            for q, (sr, si) in enumerate(sections):
                rows = pl.ds(q * FOLD, FOLD)
                tc, ts = twiddle[0, rows, cols], twiddle[1, rows, cols]
                twisted[0, rows, cols] = (sr * tc - si * ts).astype(jnp.bfloat16)
                twisted[1, rows, cols] = (sr * ts + si * tc).astype(jnp.bfloat16)
        for q in range(RADIX):
            rows = pl.ds(q * FOLD, FOLD)
            ac = jnp.dot(twisted[0, rows, :], second[...], preferred_element_type=jnp.float32)
            db = jnp.dot(twisted[1, rows, :], second[...], preferred_element_type=jnp.float32)
            a, c, dd, b = ac[:, :HALF], ac[:, HALF:], db[:, :HALF], db[:, HALF:]
            ad, bc = a * a + dd * dd, b * b + c * c
            both = ad + bc
            cross = 2.0 * (c * dd - a * b)
            lane = lax.broadcasted_iota(jnp.int32, both.shape, 1)
            edge = lane == 0
            both, cross = jnp.where(edge, 0.5 * both, both), jnp.where(edge, 0.5 * (ad - bc), cross)

            @pl.when(d == 0)
            def _():
                total_q[rows, :] = both
                total_r[rows, :] = cross

            @pl.when(d > 0)
            def _():
                total_q[rows, :] += both
                total_r[rows, :] += cross
        return 0

    lax.fori_loop(0, dets, one_detector, 0)

    def largest(i, acc):
        rows = pl.ds(pl.multiple_of(i * 32, 32), 32)
        return jnp.maximum(acc, total_q[rows, :] + jnp.abs(total_r[rows, :]))

    return jnp.max(lax.fori_loop(0, ROWS // 32, largest, jnp.zeros((32, HALF), jnp.float32)))


def body(width, strain_slots, templates, cutoffs, lists, owner, slides):
    n, groups = lax.axis_size("tpl"), lax.axis_size("grp")
    depth = n // 2 // width
    dets, bins = strain_slots.shape[1], strain_slots.shape[3]
    blocks = bins // LANES
    strain = strain_slots[0].reshape(dets, 2, blocks, LANES).transpose(0, 2, 1, 3).reshape(dets, 2 * blocks, LANES)
    count, shard = templates.shape[0], templates.shape[2]
    bank = templates.reshape(count, 2, shard // LANES, LANES).transpose(0, 2, 1, 3)
    bank = bank.reshape(count, 2 * shard // LANES, LANES)
    slots = lists.shape[1]
    first, twiddle, second = constant_tables()
    smem = pl.BlockSpec(memory_space=pltpu.SMEM)
    hbm = pl.BlockSpec(memory_space=pltpu.HBM)
    dma = pltpu.SemaphoreType.DMA
    out = jax.ShapeDtypeStruct((slots,), jnp.float32)
    half, bf16, f32 = blocks, jnp.bfloat16, jnp.float32
    prow = half // (width * depth)
    hrow = bank.shape[1] // groups
    return pl.pallas_call(
        functools.partial(kernel, width),
        out_shape=(out, out),
        in_specs=[smem] * 4 + [hbm] * 5,
        out_specs=(smem, smem),
        scratch_shapes=[
            pltpu.VMEM((dets, half, LANES), bf16),
            pltpu.VMEM((dets, half, LANES), bf16),
            pltpu.VMEM((dets, depth, prow, LANES), bf16),
            pltpu.VMEM((dets, depth, prow, LANES), bf16),
            pltpu.VMEM((2, dets, depth, prow, LANES), bf16),
            pltpu.VMEM((dets, 2 * half, LANES), bf16),
            pltpu.VMEM(bank.shape, bf16),
            pltpu.VMEM((slots, n, hrow, LANES), bf16),
            pltpu.VMEM((slots, n, bank.shape[1], LANES), bf16),
            pltpu.VMEM((TALL, LANES), f32),
            pltpu.VMEM((dets, 2, FOLD, LANES), f32),
            pltpu.VMEM((dets, 2, 8, WIDE), f32),
            pltpu.VMEM((dets, 2, FOLD, WIDE), f32),
            pltpu.VMEM((2, FOLD, WIDE), f32),
            pltpu.VMEM((2, ROWS, COLS), bf16),
            pltpu.VMEM((ROWS, HALF), f32),
            pltpu.VMEM((ROWS, HALF), f32),
            pltpu.VMEM(first.shape, bf16),
            pltpu.VMEM(twiddle.shape, f32),
            pltpu.VMEM(second.shape, bf16),
            dma((5,)),
            dma((dets, width * depth)), dma((dets, width * depth)),
            dma((dets, depth)), dma((dets, depth)),
            dma((2, dets, depth)), dma((2, dets, depth)),
            dma((2, dets, depth)), dma((2, dets, depth)),
            dma((dets, depth)), dma((dets, depth)),
            dma((dets, width * depth)), dma((dets, width * depth)),
            dma((slots, n)), dma((slots, n)),
            dma((slots, max(1, groups - 1), n)), dma((slots, max(1, groups - 1), n)),
        ],
        compiler_params=pltpu.CompilerParams(
            collective_id=0, has_side_effects=True, vmem_limit_bytes=56 * 1024 * 1024
        ),
        name="search",
    )(
        lists.T, owner, cutoffs, slides, strain, bank,
        jnp.asarray(first), jnp.asarray(twiddle), jnp.asarray(second),
    )


def solution(mesh):
    in_specs = (
        P(("grp", "tpl"), None, None, None),
        P(None, None, "tpl"),
        P(),
        P(),
        P("grp"),
        P("grp"),
    )
    out_specs = (P(("grp", "tpl")), P(("grp", "tpl")))
    width = len({d.coords[1] for d in mesh.devices[0].flat})
    return jax.shard_map(
        functools.partial(body, width), mesh=mesh, in_specs=in_specs, out_specs=out_specs, check_vma=False
    )
```

time: 108 us -> 99.3 us (0.919)
  local copies, waits for them, and re-layouts: 13.1 us -> 2.25 us
  Pallas kernels: 91.8 us -> 95.6 us
  other arithmetic: 1.13 us -> 0 us
    reshape x2 -> x0, local copies, waits for them, and re-layouts: 4.56 us -> none  [the longest x1 4.47 us: body(): bank = templates.reshape(-1, 2, rows, WIDE)]
    another operation x1 -> x0, local copies, waits for them, and re-layouts: 4.51 us -> none  [body(): strain = strain_slots[0].reshape(dets * 2, FOLD, WIDE)]
    pallas_call x2 -> x1, Pallas kernels: 91.8 us -> 95.6 us  [body(): pl.pallas_call(functools.partial(kernel, width), out_shape=(out, out), in...]
    unnamed x13 -> x2, local copies, waits for them, and re-layouts: 2.37 us -> 2.25 us
where the time goes in v1:
time: 99.3 us; the launch traced here: 99.1 us
  Pallas kernels  95.6 us (96%)
  local copies, waits for them, and re-layouts  2.25 us (2%)
  between operations  1.29 us (1%)
    pallas_call x1, Pallas kernels, body(): pl.pallas_call(functools.partial(kernel, width), out_shape=(out, out), in...  95.6 us
    unnamed x2, local copies, waits for them, and re-layouts  2.25 us

profile of v1, /device:TPU:0, one launch (start us, length us, event | category | flops | bytes accessed | tf_op | source)
XLA Modules:
  0.0 99.1 jit_solution(12356958500160354533)
XLA Ops:
  1.3 95.6 %search.1 = (f32[2]{0:T(128)}, f32[2]{0:T(128)}) custom-call(s32[2,16]{1,0:T(2,128)} %bitcast.13, s32[1]{0:T(128)S(6)} %copy.15.owner, s32[32]{0:T(128)} %cutoffs.1, s32[3]{0:T(128)} %slides.1, bf16[3,4096,128]{2,1,0:T(8,128)(2,1)} %bitcast.11, bf16[32,256,128]{2,1,0:T(8,128)(2,1)} %bitcast.12, bf16[4,256,256]{2,1,0:T(8,128)(2,1)} %constant.6.clone.first_hbm, ...), custom_call_target="tpu_custom_call" | custom-call | tf_op jit(solution)/shard_map/search/pallas_call | solution.py:552
  96.8 1.1 %copy.16 = f32[2]{0:T(128)} copy(f32[2]{0:T(128)} %get-tuple-element.4) | data formatting | bytes 16
  97.9 1.1 %copy.17 = f32[2]{0:T(128)} copy(f32[2]{0:T(128)} %get-tuple-element.5) | data formatting | bytes 16

commit v2 on v1

v2 whole, which is shorter than its diff:
```python
import jax
import jax.numpy as jnp
import numpy as np
from jax import lax
from jax.experimental import pallas as pl
from jax.experimental.pallas import tpu as pltpu
from jax.sharding import PartitionSpec as P

ROWS = 512
COLS = 512
RADIX = 4
FOLD = ROWS // RADIX
WIDE = RADIX * COLS
HALF = COLS // 2
LANES = 128
CHUNKS = WIDE // LANES
TALL = 2 * FOLD * CHUNKS

two_pi = 6.283185307179586
eps_norm = 1e-06

MESH = pl.DeviceIdType.MESH
CUT = 2
CROSS_LAG = 2
PER_STEP = 4


def turn_table(left_ids, right_ids, period):
    product_idx = left_ids[:, None] * right_ids[None, :] % period
    angles = product_idx.astype(np.float32) * np.float32(two_pi / period)
    return np.cos(angles), np.sin(angles)


def constant_tables():
    ids = np.arange(ROWS, dtype=np.int32)
    cos, sin = turn_table(ids[:FOLD], ids, ROWS)
    first = []
    for r in range(RADIX):
        c, s = cos[:, r::RADIX], sin[:, r::RADIX]
        first.append(np.concatenate([np.concatenate([c, -s], 1), np.concatenate([s, c], 1)], 0))
    twiddle = np.stack(turn_table(ids, ids, ROWS * COLS))
    cos, sin = turn_table(ids, ids[: HALF + 1], COLS)
    sin = sin[:, :HALF].copy()
    sin[:, 0] = cos[:, HALF]
    second = np.concatenate([cos[:, :HALF], sin], 1)
    return np.stack(first).astype(jnp.bfloat16), twiddle, second.astype(jnp.bfloat16)


def kernel(
    lists, owner, cutoffs, slides, strain, bank_hbm, first_hbm, twiddle_hbm, second_hbm,
    results,
    cand, other, heap, full, bank, picked, arrived, flat, row_phase, col_phase,
    turned, masked, twisted, total_q, total_r, squares, first, twiddle, second,
    local_sem, near_sem, core_send, core_recv, rs_send, rs_recv, ag_send, ag_recv,
    part_send, part_recv, swap_send, swap_recv, cross_send, cross_recv,
):
    n, groups = lax.axis_size("tpl"), lax.axis_size("grp")
    me, group = lax.axis_index("tpl"), lax.axis_index("grp")
    bits = n.bit_length() - 2
    core, chip = me % 2, me // 2
    dets = strain.shape[0] // (2 * CUT)
    units = dets * CUT
    half = strain.shape[1]
    slots = lists.shape[0]
    shard = bank.shape[1]
    hrow = shard // groups

    own_id = owner[0]
    own_chip = own_id // 2
    i_own = own_id == me

    bit = [chip // (1 << k) % 2 for k in range(bits)]
    base = [0]
    for k in range(bits):
        base.append(base[k] + bit[k] * (half >> (k + 1)))

    def flip(mask):
        return me + sum((mask & b) - 2 * (mask & b) * (me // b % 2) for b in (1 << i for i in range(n.bit_length() - 1)) if mask & b)

    partner = flip(1)
    peers = [flip(2 << k) for k in range(bits)]

    def remote(src, dst, send, recv, **where):
        return pltpu.make_async_remote_copy(
            src_ref=src, dst_ref=dst, send_sem=send, recv_sem=recv, device_id=where, device_id_type=MESH
        )

    def rows(start, size):
        return pl.ds(pl.multiple_of(start, 16), size)

    def core_copy(u):
        return remote(strain.at[2 * u + 1 - core], other.at[u], core_send.at[u], core_recv.at[u], tpl=partner)

    def away(k):
        size = half >> (k + 1)
        return rows(base[k] + (1 - bit[k]) * size, size)

    def kept(k):
        return rows(base[k], half >> k)

    def pile(k):
        return pl.ds(half - (half >> k), half >> (k + 1))

    def rs_copy(u, k):
        return remote(
            cand.at[u, away(k)], heap.at[u, pile(k)], rs_send.at[k, u], rs_recv.at[k, u], tpl=peers[k]
        )

    def ag_copy(u, k):
        at = full.at[2 * u + core, kept(k + 1)]
        return remote(at, at, ag_send.at[k, u], ag_recv.at[k, u], tpl=peers[k])

    def ag_arrival(u, k):
        at = full.at[2 * u + core, away(k)]
        return remote(at, at, ag_send.at[k, u], ag_recv.at[k, u], tpl=peers[k])

    def part_copy(u, cc, which):
        at = full.at[2 * u + cc, kept(1) if which == 0 else away(0)]
        return remote(at, at, part_send.at[which, u], part_recv.at[which, u], tpl=partner)

    def swap_peer(i):
        to = 0
        for b in (1 << e for e in range(n.bit_length() - 1)):
            to = to + (i // b % 2 + me // b % 2) % 2 * b
        return to

    def swap_copy(slot, i):
        to = swap_peer(i)
        return remote(
            picked.at[slot, to], arrived.at[slot, me, rows(group * hrow, hrow)],
            swap_send.at[slot, i], swap_recv.at[slot, i], tpl=to,
        )

    def swap_arrival(slot, i):
        source = swap_peer(i)
        return remote(
            picked.at[slot, me], arrived.at[slot, source, rows(group * hrow, hrow)],
            swap_send.at[slot, i], swap_recv.at[slot, i], tpl=source,
        )

    def cross_copy(slot, i, g):
        at = arrived.at[slot, swap_peer(i), rows(group * hrow, hrow)]
        return remote(
            at, at, cross_send.at[slot, g - 1, i], cross_recv.at[slot, g - 1, i], grp=(group + g) % groups
        )

    def cross_arrival(slot, i, g):
        source = (group - g + groups) % groups
        at = arrived.at[slot, swap_peer(i), rows(source * hrow, hrow)]
        return remote(at, at, cross_send.at[slot, g - 1, i], cross_recv.at[slot, g - 1, i], grp=source)

    tables = [
        pltpu.make_async_copy(first_hbm, first, local_sem.at[2]),
        pltpu.make_async_copy(twiddle_hbm, twiddle, local_sem.at[3]),
        pltpu.make_async_copy(second_hbm, second, local_sem.at[4]),
    ]
    mine_copies = [
        pltpu.make_async_copy(strain.at[2 * u + core], cand.at[u], local_sem.at[5 + u]) for u in range(units)
    ]
    bank_copy = pltpu.make_async_copy(bank_hbm, bank, local_sem.at[0])
    for copy in mine_copies:
        copy.start()
    bank_copy.start()

    barrier = pltpu.get_barrier_semaphore()
    for peer in [partner] + peers:
        pl.semaphore_signal(barrier, inc=1, device_id={"tpl": peer}, device_id_type=MESH)
    for g in range(1, groups):
        pl.semaphore_signal(barrier, inc=1, device_id={"grp": (group + g) % groups}, device_id_type=MESH)
    make_phases(slides, row_phase, col_phase)
    pl.semaphore_wait(barrier, bits + groups)

    for u in range(units):
        core_copy(u).start()

    def greet(k):
        pl.semaphore_signal(near_sem.at[k], inc=1, device_id={"tpl": ([partner] + peers)[k]}, device_id_type=MESH)

    def choice(u, where):
        cand[u, where] = jnp.where(i_own, cand[u, where], other[u, where])

    greet(0)
    for u in range(units):
        mine_copies[u].wait()
        core_copy(u).wait_recv()
        choice(u, away(0))
        rs_copy(u, 0).start()
        choice(u, kept(1))
        if u < bits:
            pl.semaphore_wait(near_sem.at[u], 1)
            if u + 1 < bits:
                greet(u + 1)
    for u in range(units, bits):
        pl.semaphore_wait(near_sem.at[u], 1)
        if u + 1 < bits:
            greet(u + 1)
    for copy in tables:
        copy.start()
    bank_copy.wait()
    for slot in range(slots):
        arrived[slot, me] = bank[lists[slot, me]]

    def merge(u, k, where, start, size):
        agree = own_chip // (1 << k) == chip // (1 << k)
        offset = half - (half >> k) + start - base[k + 1]
        return jnp.where(agree, cand[u, where], heap[u, rows(offset, size)])

    def stage(u, e):
        if e < bits:
            k = e
            rs_copy(u, k).wait_recv()
            if k + 1 < bits:
                size = half >> (k + 2)
                start = base[k + 1] + (1 - bit[k + 1]) * size
                cand[u, away(k + 1)] = merge(u, k, away(k + 1), start, size)
                rs_copy(u, k + 1).start()
                cand[u, kept(k + 2)] = merge(u, k, kept(k + 2), base[k + 2], size)
            else:
                full[2 * u + core, kept(bits)] = merge(u, k, kept(bits), base[bits], half >> bits)
                ag_copy(u, bits - 1).start()
        else:
            k = 2 * bits - 1 - e
            ag_arrival(u, k).wait_recv()
            if k > 0:
                ag_copy(u, k - 1).start()
            if k < 2:
                part_copy(u, core, 1 - k).start()

    messages = slots * (n - 1)
    per_step = max(PER_STEP, -(-messages // (units + 2 * bits - CROSS_LAG)))
    landed = [((n - 1) * (slot + 1) - 1) // per_step + CROSS_LAG for slot in range(slots)]
    turn_at = [u + 2 * bits for u in range(units)]
    clock = 0
    mask_at, filter_at = [], []
    for slot in range(slots):
        mask_at.append(landed[slot] + 1)
    pairs = sorted(
        (max(turn_at[CUT * (d + 1) - 1], mask_at[slot]), d, slot) for d in range(dets) for slot in range(slots)
    )
    for ready, d, slot in pairs:
        clock = max(clock + 1, ready)
        filter_at.append((clock, slot, d))
    steps = max(clock, units + 2 * bits, per_step) + 1

    def swap_start(q):
        slot, i = q // (n - 1), n - 1 - q % (n - 1)
        to = swap_peer(i)
        picked[slot, to] = bank[lists[slot, to], rows(group * hrow, hrow)]
        swap_copy(slot, i).start()

    def cross_start(q):
        slot, i = q // (n - 1), n - 1 - q % (n - 1)
        swap_arrival(slot, i).wait_recv()
        for g in range(1, groups):
            cross_copy(slot, i, g).start()

    def choose(t, pairs):
        value, hit = 0, False
        for at, v in pairs:
            value, hit = jnp.where(t == at, v, value), (t == at) | hit
        return value, hit

    def step_body(t, _):
        for e in range(2 * bits):
            u = t - e

            @pl.when((u >= 0) & (u < units))
            def _():
                stage(u, e)

        for e in range(per_step):
            q = t * per_step + e

            @pl.when(q < messages)
            def _():
                swap_start(q)

            p = (t - CROSS_LAG) * per_step + e

            @pl.when((p >= 0) & (p < messages))
            def _():
                cross_start(p)

        u, now = choose(t, list(zip(turn_at, range(units))))

        @pl.when(now)
        def _():
            for which in range(2):
                part_arrival(u, which).wait_recv()
            turn_unit(full.at[pl.ds(2 * u, 2)], flat, row_phase, col_phase, turned, u // CUT, u % CUT)

        slot, now = choose(t, list(zip(mask_at, range(slots))))

        @pl.when(now)
        def _():
            def join(i, _):
                for g in range(1, groups):
                    cross_arrival(slot, i, g).wait_recv()
                return 0

            lax.fori_loop(1, n, join, 0)
            cutoff = cutoffs[lists[slot, me]]
            squares[slot] = mask_template(cutoff, arrived.at[slot], flat, masked.at[slot])

        pair, now = choose(t, [(at, slot * dets + d) for at, slot, d in filter_at])

        @pl.when(now)
        def _():
            slot, d = pair // dets, pair % dets
            filter_detector(
                d, turned.at[d], masked.at[slot], first, twiddle, second, twisted,
                total_q.at[slot], total_r.at[slot],
            )

        return 0

    def part_arrival(u, which):
        at = full.at[2 * u + 1 - core, kept(1) if which == 0 else away(0)]
        return remote(at, at, part_send.at[which, u], part_recv.at[which, u], tpl=partner)

    for copy in tables:
        copy.wait()
    lax.fori_loop(0, steps, step_body, 0)

    def drain(u, _):
        core_copy(u).wait_send()
        for k in range(bits):
            rs_copy(u, k).wait_send()
            ag_copy(u, k).wait_send()
        for which in range(2):
            part_copy(u, core, which).wait_send()
        return 0

    lax.fori_loop(0, units, drain, 0)

    def finish_swap(i, _):
        for slot in range(slots):
            swap_copy(slot, i).wait_send()
            for g in range(1, groups):
                cross_copy(slot, i, g).wait_send()
        return 0

    lax.fori_loop(1, n, finish_swap, 0)
    for slot in range(slots):
        sigmasq = jnp.sum(squares[slot])
        results[slot] = largest(total_q.at[slot], total_r.at[slot]) / (2.0 * (sigmasq + eps_norm))
        results[slots + slot] = sigmasq / (ROWS * COLS)


def make_phases(slides, row_phase, col_phase):
    total = ROWS * COLS
    for d in range(row_phase.shape[0]):
        slide = slides[d]
        row = lax.broadcasted_iota(jnp.int32, (FOLD, LANES), 0) * slide % FOLD
        row = row.astype(jnp.float32) * (two_pi / FOLD)
        row_phase[d, 0] = jnp.cos(row)
        row_phase[d, 1] = jnp.sin(row)
        col = lax.broadcasted_iota(jnp.int32, (8, WIDE), 1) * slide % total
        col = col.astype(jnp.float32) * (two_pi / total)
        col_phase[d, 0] = jnp.cos(col)
        col_phase[d, 1] = jnp.sin(col)


def tile(flat, i, c, part):
    return flat[pl.ds((i * 8 * CHUNKS + c) * 2 + part, 8, stride=2 * CHUNKS), :]


def turn_unit(source, flat, row_phase, col_phase, turned, d, q):
    half, size = source.shape[1], 256
    high = FOLD // CUT

    def widen(i, _):
        for h in range(2):
            at = pl.ds(pl.multiple_of(i * size, size), size)
            flat[pl.ds(pl.multiple_of(h * half + i * size, size), size), :] = source[h, at, :].astype(jnp.float32)
        return 0

    lax.fori_loop(0, half // size, widen, 0)

    def body(i, _):
        at = pl.ds(pl.multiple_of(q * high + i * 8, 8), 8)
        rr, ri = row_phase[d, 0, at, :], row_phase[d, 1, at, :]
        for c in range(CHUNKS):
            cols = pl.ds(c * LANES, LANES)
            cr, ci = col_phase[d, 0, :, cols], col_phase[d, 1, :, cols]
            pr, pi = rr * cr - ri * ci, rr * ci + ri * cr
            xr, xi = tile(flat, i, c, 0), tile(flat, i, c, 1)
            turned[d, 0, at, cols] = xr * pr - xi * pi
            turned[d, 1, at, cols] = xr * pi + xi * pr
        return 0

    lax.fori_loop(0, high // 8, body, 0)


def mask_template(cutoff, source, flat, masked):
    shards, shard = source.shape[0], source.shape[1]

    def body(i, _):
        flat[pl.ds(pl.multiple_of(i * shard, shard), shard), :] = source[i].astype(jnp.float32)
        return 0

    lax.fori_loop(0, shards, body, 0)

    def mask(i, acc):
        at = pl.ds(pl.multiple_of(i * 8, 8), 8)
        base = (lax.broadcasted_iota(jnp.int32, (8, LANES), 0) + i * 8) * WIDE + lax.broadcasted_iota(
            jnp.int32, (8, LANES), 1
        )
        for c in range(CHUNKS):
            cols = pl.ds(c * LANES, LANES)
            inside = base < cutoff - c * LANES
            wr = jnp.where(inside, tile(flat, i, c, 0), 0.0)
            wi = jnp.where(inside, tile(flat, i, c, 1), 0.0)
            masked[0, at, cols] = wr
            masked[1, at, cols] = wi
            acc = acc + (wr * wr + wi * wi)
        return acc

    return lax.fori_loop(0, FOLD // 8, mask, jnp.zeros((8, LANES), jnp.float32))


def filter_detector(d, turned, masked, first, twiddle, second, twisted, total_q, total_r):
    for c in range(COLS // 256):
        parts = []
        for r in range(RADIX):
            cols = pl.ds(r * COLS + c * 256, 256)
            xr, xi = turned[0, :, cols], turned[1, :, cols]
            wr, wi = masked[0, :, cols], masked[1, :, cols]
            product = jnp.concatenate([xr * wr + xi * wi, xi * wr - xr * wi], 0)
            out = jnp.dot(first[r], product.astype(jnp.bfloat16), preferred_element_type=jnp.float32)
            parts.append((out[:FOLD], out[FOLD:]))
        (r0, i0), (r1, i1), (r2, i2), (r3, i3) = parts
        ar, ai, br, bi = r0 + r2, i0 + i2, r0 - r2, i0 - i2
        cr, ci, dr, di = r1 + r3, i1 + i3, i3 - i1, r1 - r3
        sections = (
            (ar + cr, ai + ci), (br + dr, bi + di), (ar - cr, ai - ci), (br - dr, bi - di)
        )
        cols = pl.ds(c * 256, 256)
        for q, (sr, si) in enumerate(sections):
            rows = pl.ds(q * FOLD, FOLD)
            tc, ts = twiddle[0, rows, cols], twiddle[1, rows, cols]
            twisted[0, rows, cols] = (sr * tc - si * ts).astype(jnp.bfloat16)
            twisted[1, rows, cols] = (sr * ts + si * tc).astype(jnp.bfloat16)
    for q in range(RADIX):
        rows = pl.ds(q * FOLD, FOLD)
        ac = jnp.dot(twisted[0, rows, :], second[...], preferred_element_type=jnp.float32)
        db = jnp.dot(twisted[1, rows, :], second[...], preferred_element_type=jnp.float32)
        a, c, dd, b = ac[:, :HALF], ac[:, HALF:], db[:, :HALF], db[:, HALF:]
        ad, bc = a * a + dd * dd, b * b + c * c
        both = ad + bc
        cross = 2.0 * (c * dd - a * b)
        lane = lax.broadcasted_iota(jnp.int32, both.shape, 1)
        edge = lane == 0
        both, cross = jnp.where(edge, 0.5 * both, both), jnp.where(edge, 0.5 * (ad - bc), cross)

        @pl.when(d == 0)
        def _():
            total_q[rows, :] = both
            total_r[rows, :] = cross

        @pl.when(d > 0)
        def _():
            total_q[rows, :] += both
            total_r[rows, :] += cross

def largest(total_q, total_r):
    def body(i, acc):
        rows = pl.ds(pl.multiple_of(i * 32, 32), 32)
        return jnp.maximum(acc, total_q[rows, :] + jnp.abs(total_r[rows, :]))

    return jnp.max(lax.fori_loop(0, ROWS // 32, body, jnp.zeros((32, HALF), jnp.float32)))


def body(strain_slots, templates, cutoffs, lists, owner, slides):
    n, groups = lax.axis_size("tpl"), lax.axis_size("grp")
    bits = n.bit_length() - 2
    dets, bins = strain_slots.shape[1], strain_slots.shape[3]
    units, half = dets * CUT, bins // LANES // CUT
    strain = strain_slots[0].reshape(dets, 2, bins // LANES, LANES).transpose(0, 2, 1, 3)
    strain = strain.reshape(2 * units, half, LANES)
    count, shard = templates.shape[0], templates.shape[2]
    bank = templates.reshape(count, 2, shard // LANES, LANES).transpose(0, 2, 1, 3)
    bank = bank.reshape(count, 2 * shard // LANES, LANES)
    slots = lists.shape[1]
    first, twiddle, second = constant_tables()
    smem = pl.BlockSpec(memory_space=pltpu.SMEM)
    hbm = pl.BlockSpec(memory_space=pltpu.HBM)
    dma, bf16, f32 = pltpu.SemaphoreType.DMA, jnp.bfloat16, jnp.float32
    hrow = bank.shape[1] // groups
    results = pl.pallas_call(
        kernel,
        out_shape=jax.ShapeDtypeStruct((2 * slots,), f32),
        in_specs=[smem] * 4 + [hbm] * 5,
        out_specs=smem,
        scratch_shapes=[
            pltpu.VMEM((units, half, LANES), bf16),
            pltpu.VMEM((units, half, LANES), bf16),
            pltpu.VMEM((units, half, LANES), bf16),
            pltpu.VMEM((2 * units, half, LANES), bf16),
            pltpu.VMEM(bank.shape, bf16),
            pltpu.VMEM((slots, n, hrow, LANES), bf16),
            pltpu.VMEM((slots, n, bank.shape[1], LANES), bf16),
            pltpu.VMEM((TALL, LANES), f32),
            pltpu.VMEM((dets, 2, FOLD, LANES), f32),
            pltpu.VMEM((dets, 2, 8, WIDE), f32),
            pltpu.VMEM((dets, 2, FOLD, WIDE), f32),
            pltpu.VMEM((slots, 2, FOLD, WIDE), f32),
            pltpu.VMEM((2, ROWS, COLS), bf16),
            pltpu.VMEM((slots, ROWS, HALF), f32),
            pltpu.VMEM((slots, ROWS, HALF), f32),
            pltpu.VMEM((slots, 8, LANES), f32),
            pltpu.VMEM(first.shape, bf16),
            pltpu.VMEM(twiddle.shape, f32),
            pltpu.VMEM(second.shape, bf16),
            dma((5 + units,)),
            pltpu.SemaphoreType.REGULAR((bits,)),
            dma((units,)), dma((units,)),
            dma((bits, units)), dma((bits, units)),
            dma((bits, units)), dma((bits, units)),
            dma((2, units)), dma((2, units)),
            dma((slots, n)), dma((slots, n)),
            dma((slots, max(1, groups - 1), n)), dma((slots, max(1, groups - 1), n)),
        ],
        compiler_params=pltpu.CompilerParams(
            collective_id=0, has_side_effects=True, vmem_limit_bytes=56 * 1024 * 1024
        ),
        name="search",
    )(
        lists.T, owner, cutoffs, slides, strain, bank,
        jnp.asarray(first), jnp.asarray(twiddle), jnp.asarray(second),
    )
    return results[:slots], results[slots:]


def solution(mesh):
    in_specs = (
        P(("grp", "tpl"), None, None, None),
        P(None, None, "tpl"),
        P(),
        P(),
        P("grp"),
        P("grp"),
    )
    out_specs = (P(("grp", "tpl")), P(("grp", "tpl")))
    return jax.shard_map(body, mesh=mesh, in_specs=in_specs, out_specs=out_specs, check_vma=False)
```

time: 99.3 us -> 84.6 us (0.85)
  Pallas kernels: 95.6 us -> 81.9 us
    pallas_call x1, Pallas kernels: 95.6 us -> 81.9 us  [body(): pl.pallas_call(kernel, out_shape=jax.ShapeDtypeStruct((2 * slots,), f32),...]
    unnamed x2 -> x0, local copies, waits for them, and re-layouts: 2.25 us -> none
    slice x0 -> x1, local copies, waits for them, and re-layouts: none -> 1.26 us  [body(): return (results[:slots], results[slots:])]
where the time goes in v2:
time: 84.6 us; the launch traced here: 84.4 us
  Pallas kernels  81.9 us (97%)
  between operations  1.29 us (2%)
  local copies, waits for them, and re-layouts  1.26 us (1%)
    pallas_call x1, Pallas kernels, body(): pl.pallas_call(kernel, out_shape=jax.ShapeDtypeStruct((2 * slots,), f32),...  81.9 us

profile of v2, /device:TPU:0, one launch (start us, length us, event | category | flops | bytes accessed | tf_op | source)
XLA Modules:
  0.0 84.4 jit_solution(11173413779987935289)
XLA Ops:
  1.3 81.9 %search.1 = f32[4]{0:T(128)} custom-call(s32[2,16]{1,0:T(2,128)} %bitcast.13, s32[1]{0:T(128)S(6)} %copy.13.owner, s32[32]{0:T(128)} %cutoffs.1, s32[3]{0:T(128)} %slides.1, bf16[12,1024,128]{2,1,0:T(8,128)(2,1)} %bitcast.11, bf16[32,256,128]{2,1,0:T(8,128)(2,1)} %bitcast.12, bf16[4,256,256]{2,1,0:T(8,128)(2,1)} %constant.6.clone.first_hbm, ...), custom_call_target="tpu_custom_call" | custom-call | tf_op jit(solution)/shard_map/search/pallas_call | solution.py:490
  83.2 1.3 %fusion = (f32[2]{0:T(128)}, f32[2]{0:T(128)}) fusion(f32[4]{0:T(128)} %search.1), kind=kLoop, calls=%fused_computation | loop fusion | bytes 32 | tf_op jit(solution)/shard_map/slice | solution.py:532

commit v3 on v2

--- a/solution.py
+++ b/solution.py
@@ -21,8 +21,10 @@
 
 MESH = pl.DeviceIdType.MESH
 CUT = 2
-CROSS_LAG = 2
-PER_STEP = 4
+EARLY = 8
+SWAP_STEP = 4
+CROSS_STEP = 5
+CROSS_FROM = 1
 
 
 def turn_table(left_ids, right_ids, period):
@@ -50,7 +52,7 @@
     lists, owner, cutoffs, slides, strain, bank_hbm, first_hbm, twiddle_hbm, second_hbm,
     results,
     cand, other, heap, full, bank, picked, arrived, flat, row_phase, col_phase,
-    turned, masked, twisted, total_q, total_r, squares, first, twiddle, second,
+    turned, masked, twisted, sections, total_q, total_r, squares, first, twiddle, second,
     local_sem, near_sem, core_send, core_recv, rs_send, rs_recv, ag_send, ag_recv,
     part_send, part_recv, swap_send, swap_recv, cross_send, cross_recv,
 ):
@@ -74,8 +76,10 @@
     for k in range(bits):
         base.append(base[k] + bit[k] * (half >> (k + 1)))
 
+    turns = [(1 << k) * (1 - 2 * (me // (1 << k) % 2)) for k in range(bits + 1)]
+
     def flip(mask):
-        return me + sum((mask & b) - 2 * (mask & b) * (me // b % 2) for b in (1 << i for i in range(n.bit_length() - 1)) if mask & b)
+        return me + sum(turns[k] for k in range(bits + 1) if mask >> k & 1)
 
     partner = flip(1)
     peers = [flip(2 << k) for k in range(bits)]
@@ -89,7 +93,7 @@
         return pl.ds(pl.multiple_of(start, 16), size)
 
     def core_copy(u):
-        return remote(strain.at[2 * u + 1 - core], other.at[u], core_send.at[u], core_recv.at[u], tpl=partner)
+        return remote(strain.at[2 * u + 1 - core], other.at[u], core_send, core_recv.at[u], tpl=partner)
 
     def away(k):
         size = half >> (k + 1)
@@ -103,51 +107,46 @@
 
     def rs_copy(u, k):
         return remote(
-            cand.at[u, away(k)], heap.at[u, pile(k)], rs_send.at[k, u], rs_recv.at[k, u], tpl=peers[k]
+            cand.at[u, away(k)], heap.at[u, pile(k)], rs_send, rs_recv.at[k, u], tpl=peers[k]
         )
 
     def ag_copy(u, k):
         at = full.at[2 * u + core, kept(k + 1)]
-        return remote(at, at, ag_send.at[k, u], ag_recv.at[k, u], tpl=peers[k])
+        return remote(at, at, ag_send, ag_recv.at[k, u], tpl=peers[k])
 
     def ag_arrival(u, k):
         at = full.at[2 * u + core, away(k)]
-        return remote(at, at, ag_send.at[k, u], ag_recv.at[k, u], tpl=peers[k])
+        return remote(at, at, ag_send, ag_recv.at[k, u], tpl=peers[k])
 
     def part_copy(u, cc, which):
         at = full.at[2 * u + cc, kept(1) if which == 0 else away(0)]
-        return remote(at, at, part_send.at[which, u], part_recv.at[which, u], tpl=partner)
-
-    def swap_peer(i):
-        to = 0
-        for b in (1 << e for e in range(n.bit_length() - 1)):
-            to = to + (i // b % 2 + me // b % 2) % 2 * b
-        return to
+        return remote(at, at, part_send, part_recv.at[which, u], tpl=partner)
 
     def swap_copy(slot, i):
-        to = swap_peer(i)
+        to = flip(i)
         return remote(
             picked.at[slot, to], arrived.at[slot, me, rows(group * hrow, hrow)],
-            swap_send.at[slot, i], swap_recv.at[slot, i], tpl=to,
+            swap_send, swap_recv.at[slot, i], tpl=to,
         )
 
     def swap_arrival(slot, i):
-        source = swap_peer(i)
+        source = flip(i)
         return remote(
             picked.at[slot, me], arrived.at[slot, source, rows(group * hrow, hrow)],
-            swap_send.at[slot, i], swap_recv.at[slot, i], tpl=source,
+            swap_send, swap_recv.at[slot, i], tpl=source,
         )
 
     def cross_copy(slot, i, g):
-        at = arrived.at[slot, swap_peer(i), rows(group * hrow, hrow)]
+        at = arrived.at[slot, flip(i), rows(group * hrow, hrow)]
         return remote(
-            at, at, cross_send.at[slot, g - 1, i], cross_recv.at[slot, g - 1, i], grp=(group + g) % groups
-        )
-
-    def cross_arrival(slot, i, g):
-        source = (group - g + groups) % groups
-        at = arrived.at[slot, swap_peer(i), rows(source * hrow, hrow)]
-        return remote(at, at, cross_send.at[slot, g - 1, i], cross_recv.at[slot, g - 1, i], grp=source)
+            at, at, cross_send.at[g - 1], cross_recv.at[slot, g - 1], grp=(group + g) % groups
+        )
+
+    def cross_arrivals(slot, g):
+        at = picked.at[slot, pl.ds(0, n - 1)]
+        return remote(
+            at, at, cross_send.at[g - 1], cross_recv.at[slot, g - 1], grp=(group + g) % groups
+        )
 
     tables = [
         pltpu.make_async_copy(first_hbm, first, local_sem.at[2]),
@@ -167,7 +166,6 @@
         pl.semaphore_signal(barrier, inc=1, device_id={"tpl": peer}, device_id_type=MESH)
     for g in range(1, groups):
         pl.semaphore_signal(barrier, inc=1, device_id={"grp": (group + g) % groups}, device_id_type=MESH)
-    make_phases(slides, row_phase, col_phase)
     pl.semaphore_wait(barrier, bits + groups)
 
     for u in range(units):
@@ -194,11 +192,35 @@
         pl.semaphore_wait(near_sem.at[u], 1)
         if u + 1 < bits:
             greet(u + 1)
+    bank_copy.wait()
+    apart = sorted(range(2, n), key=lambda i: (i & 2, -i))
+    alone = sum(1 for i in apart if not i & 2)
+    queue = [(slot, 1) for slot in range(slots)]
+    queue += [(slot, i) for slot in range(slots) for i in apart[:alone]]
+    queue += [(slot, i) for slot in range(slots) for i in apart[alone:]]
+    early = max(0, min(EARLY, len(queue)))
+
+    def swap_start(q):
+        slot, i = queue[q]
+        to = flip(i)
+        picked[slot, to] = bank[lists[slot, to], rows(group * hrow, hrow)]
+        swap_copy(slot, i).start()
+
+    def cross_start(q):
+        slot, i = queue[q]
+        swap_arrival(slot, i).wait_recv()
+        for g in range(1, groups):
+            cross_copy(slot, i, g).start()
+
+    for q in range(early):
+        swap_start(q)
     for copy in tables:
         copy.start()
-    bank_copy.wait()
+    make_phases(slides, row_phase, col_phase)
     for slot in range(slots):
         arrived[slot, me] = bank[lists[slot, me]]
+    total_q[...] = jnp.zeros_like(total_q)
+    total_r[...] = jnp.zeros_like(total_r)
 
     def merge(u, k, where, start, size):
         agree = own_chip // (1 << k) == chip // (1 << k)
@@ -226,33 +248,25 @@
             if k < 2:
                 part_copy(u, core, 1 - k).start()
 
-    messages = slots * (n - 1)
-    per_step = max(PER_STEP, -(-messages // (units + 2 * bits - CROSS_LAG)))
-    landed = [((n - 1) * (slot + 1) - 1) // per_step + CROSS_LAG for slot in range(slots)]
+    talk = units + 2 * bits - 1
+    swap_step = max(SWAP_STEP, -(-(len(queue) - early) // (talk - 3)))
+    cross_step = max(CROSS_STEP, -(-len(queue) // (talk - CROSS_FROM)))
+    swap_slots = [range(early + t * swap_step, min(len(queue), early + (t + 1) * swap_step)) for t in range(talk)]
+    ends = [min(len(queue), (t - CROSS_FROM + 1) * cross_step, early + max(0, t - 1) * swap_step) for t in range(talk)]
+    ends = [max(0, end) if t >= CROSS_FROM else 0 for t, end in enumerate(ends)] + [len(queue)]
+    cross_slots = [range(ends[t - 1] if t else 0, ends[t]) for t in range(talk + 1)]
+    swap_slots.append(())
+    talk += 1
+    landed = [
+        max(t for t in range(talk) if any(queue[q][0] == slot for q in cross_slots[t])) for slot in range(slots)
+    ]
     turn_at = [u + 2 * bits for u in range(units)]
-    clock = 0
-    mask_at, filter_at = [], []
-    for slot in range(slots):
-        mask_at.append(landed[slot] + 1)
+    mask_at = [at + 1 for at in landed]
     pairs = sorted(
         (max(turn_at[CUT * (d + 1) - 1], mask_at[slot]), d, slot) for d in range(dets) for slot in range(slots)
     )
-    for ready, d, slot in pairs:
-        clock = max(clock + 1, ready)
-        filter_at.append((clock, slot, d))
-    steps = max(clock, units + 2 * bits, per_step) + 1
-
-    def swap_start(q):
-        slot, i = q // (n - 1), n - 1 - q % (n - 1)
-        to = swap_peer(i)
-        picked[slot, to] = bank[lists[slot, to], rows(group * hrow, hrow)]
-        swap_copy(slot, i).start()
-
-    def cross_start(q):
-        slot, i = q // (n - 1), n - 1 - q % (n - 1)
-        swap_arrival(slot, i).wait_recv()
-        for g in range(1, groups):
-            cross_copy(slot, i, g).start()
+    filter_at = [ready for ready, _, _ in pairs]
+    steps = max(filter_at[-1], units + 2 * bits, landed[-1]) + 1
 
     def choose(t, pairs):
         value, hit = 0, False
@@ -261,25 +275,16 @@
         return value, hit
 
     def step_body(t, _):
-        for e in range(2 * bits):
-            u = t - e
-
-            @pl.when((u >= 0) & (u < units))
+        for at in range(talk):
+            @pl.when(t == at)
             def _():
-                stage(u, e)
-
-        for e in range(per_step):
-            q = t * per_step + e
-
-            @pl.when(q < messages)
-            def _():
-                swap_start(q)
-
-            p = (t - CROSS_LAG) * per_step + e
-
-            @pl.when((p >= 0) & (p < messages))
-            def _():
-                cross_start(p)
+                for e in range(2 * bits):
+                    if 0 <= at - e < units:
+                        stage(at - e, e)
+                for q in cross_slots[at]:
+                    cross_start(q)
+                for q in swap_slots[at]:
+                    swap_start(q)
 
         u, now = choose(t, list(zip(turn_at, range(units))))
 
@@ -293,54 +298,44 @@
 
         @pl.when(now)
         def _():
-            def join(i, _):
-                for g in range(1, groups):
-                    cross_arrival(slot, i, g).wait_recv()
-                return 0
-
-            lax.fori_loop(1, n, join, 0)
+            for g in range(1, groups):
+                cross_arrivals(slot, g).wait_recv()
             cutoff = cutoffs[lists[slot, me]]
             squares[slot] = mask_template(cutoff, arrived.at[slot], flat, masked.at[slot])
 
-        pair, now = choose(t, [(at, slot * dets + d) for at, slot, d in filter_at])
-
-        @pl.when(now)
-        def _():
-            slot, d = pair // dets, pair % dets
+        def one_filter(f, _):
+            slot = choose(f, [(k, pair[2]) for k, pair in enumerate(pairs)])[0]
+            d = choose(f, [(k, pair[1]) for k, pair in enumerate(pairs)])[0]
             filter_detector(
-                d, turned.at[d], masked.at[slot], first, twiddle, second, twisted,
+                turned.at[d], masked.at[slot], first, twiddle, second, twisted, sections,
                 total_q.at[slot], total_r.at[slot],
             )
-
+            return 0
+
+        begin = sum((t > at).astype(jnp.int32) for at in filter_at)
+        end = sum((t >= at).astype(jnp.int32) for at in filter_at)
+        lax.fori_loop(begin, end, one_filter, 0)
         return 0
 
     def part_arrival(u, which):
         at = full.at[2 * u + 1 - core, kept(1) if which == 0 else away(0)]
-        return remote(at, at, part_send.at[which, u], part_recv.at[which, u], tpl=partner)
+        return remote(at, at, part_send, part_recv.at[which, u], tpl=partner)
 
     for copy in tables:
         copy.wait()
     lax.fori_loop(0, steps, step_body, 0)
 
-    def drain(u, _):
-        core_copy(u).wait_send()
-        for k in range(bits):
-            rs_copy(u, k).wait_send()
-            ag_copy(u, k).wait_send()
-        for which in range(2):
-            part_copy(u, core, which).wait_send()
-        return 0
-
-    lax.fori_loop(0, units, drain, 0)
-
-    def finish_swap(i, _):
-        for slot in range(slots):
-            swap_copy(slot, i).wait_send()
-            for g in range(1, groups):
-                cross_copy(slot, i, g).wait_send()
-        return 0
-
-    lax.fori_loop(1, n, finish_swap, 0)
+    def sent(at, semaphore):
+        remote(at, at, semaphore, core_recv.at[0], tpl=partner).wait_send()
+
+    walk = heap.at[:, pl.ds(0, half - (half >> bits))]
+    for at, semaphore in (
+        (other, core_send), (walk, rs_send), (walk, ag_send), (other, part_send),
+        (picked.at[:, pl.ds(0, n - 1)], swap_send),
+    ):
+        sent(at, semaphore)
+    for g in range(1, groups):
+        sent(picked.at[:, pl.ds(0, n - 1)], cross_send.at[g - 1])
     for slot in range(slots):
         sigmasq = jnp.sum(squares[slot])
         results[slot] = largest(total_q.at[slot], total_r.at[slot]) / (2.0 * (sigmasq + eps_norm))
@@ -349,7 +344,8 @@
 
 def make_phases(slides, row_phase, col_phase):
     total = ROWS * COLS
-    for d in range(row_phase.shape[0]):
+
+    def body(d, _):
         slide = slides[d]
         row = lax.broadcasted_iota(jnp.int32, (FOLD, LANES), 0) * slide % FOLD
         row = row.astype(jnp.float32) * (two_pi / FOLD)
@@ -359,6 +355,9 @@
         col = col.astype(jnp.float32) * (two_pi / total)
         col_phase[d, 0] = jnp.cos(col)
         col_phase[d, 1] = jnp.sin(col)
+        return 0
+
+    lax.fori_loop(0, row_phase.shape[0], body, 0)
 
 
 def tile(flat, i, c, part):
@@ -419,54 +418,45 @@
     return lax.fori_loop(0, FOLD // 8, mask, jnp.zeros((8, LANES), jnp.float32))
 
 
-def filter_detector(d, turned, masked, first, twiddle, second, twisted, total_q, total_r):
+def filter_detector(turned, masked, first, twiddle, second, twisted, sections, total_q, total_r):
     for c in range(COLS // 256):
-        parts = []
         for r in range(RADIX):
             cols = pl.ds(r * COLS + c * 256, 256)
             xr, xi = turned[0, :, cols], turned[1, :, cols]
             wr, wi = masked[0, :, cols], masked[1, :, cols]
             product = jnp.concatenate([xr * wr + xi * wi, xi * wr - xr * wi], 0)
-            out = jnp.dot(first[r], product.astype(jnp.bfloat16), preferred_element_type=jnp.float32)
-            parts.append((out[:FOLD], out[FOLD:]))
-        (r0, i0), (r1, i1), (r2, i2), (r3, i3) = parts
-        ar, ai, br, bi = r0 + r2, i0 + i2, r0 - r2, i0 - i2
-        cr, ci, dr, di = r1 + r3, i1 + i3, i3 - i1, r1 - r3
-        sections = (
-            (ar + cr, ai + ci), (br + dr, bi + di), (ar - cr, ai - ci), (br - dr, bi - di)
-        )
+            sections[c, r] = jnp.dot(first[r], product.astype(jnp.bfloat16), preferred_element_type=jnp.float32)
         cols = pl.ds(c * 256, 256)
-        for q, (sr, si) in enumerate(sections):
-            rows = pl.ds(q * FOLD, FOLD)
-            tc, ts = twiddle[0, rows, cols], twiddle[1, rows, cols]
-            twisted[0, rows, cols] = (sr * tc - si * ts).astype(jnp.bfloat16)
-            twisted[1, rows, cols] = (sr * ts + si * tc).astype(jnp.bfloat16)
-    for q in range(RADIX):
-        rows = pl.ds(q * FOLD, FOLD)
-        ac = jnp.dot(twisted[0, rows, :], second[...], preferred_element_type=jnp.float32)
-        db = jnp.dot(twisted[1, rows, :], second[...], preferred_element_type=jnp.float32)
-        a, c, dd, b = ac[:, :HALF], ac[:, HALF:], db[:, :HALF], db[:, HALF:]
-        ad, bc = a * a + dd * dd, b * b + c * c
-        both = ad + bc
-        cross = 2.0 * (c * dd - a * b)
-        lane = lax.broadcasted_iota(jnp.int32, both.shape, 1)
-        edge = lane == 0
-        both, cross = jnp.where(edge, 0.5 * both, both), jnp.where(edge, 0.5 * (ad - bc), cross)
-
-        @pl.when(d == 0)
-        def _():
-            total_q[rows, :] = both
-            total_r[rows, :] = cross
-
-        @pl.when(d > 0)
-        def _():
-            total_q[rows, :] += both
-            total_r[rows, :] += cross
+        for b in range(FOLD // 16):
+            r0, r1, r2, r3 = [sections[c, r, pl.ds(b * 16, 16), :] for r in range(RADIX)]
+            i0, i1, i2, i3 = [sections[c, r, pl.ds(FOLD + b * 16, 16), :] for r in range(RADIX)]
+            ar, ai, br, bi = r0 + r2, i0 + i2, r0 - r2, i0 - i2
+            cr, ci, dr, di = r1 + r3, i1 + i3, i3 - i1, r1 - r3
+            quarters = (
+                (ar + cr, ai + ci), (br + dr, bi + di), (ar - cr, ai - ci), (br - dr, bi - di)
+            )
+            for q, (sr, si) in enumerate(quarters):
+                rows = pl.ds(q * FOLD + b * 16, 16)
+                tc, ts = twiddle[0, rows, cols], twiddle[1, rows, cols]
+                twisted[0, rows, cols] = (sr * tc - si * ts).astype(jnp.bfloat16)
+                twisted[1, rows, cols] = (sr * ts + si * tc).astype(jnp.bfloat16)
+    ac = jnp.dot(twisted[0], second[...], preferred_element_type=jnp.float32)
+    db = jnp.dot(twisted[1], second[...], preferred_element_type=jnp.float32)
+    a, c, d, b = ac[:, :HALF], ac[:, HALF:], db[:, :HALF], db[:, HALF:]
+    ad, bc = a * a + d * d, b * b + c * c
+    both, cross = ad + bc, c * d - a * b
+    edge = lax.broadcasted_iota(jnp.int32, (ROWS, LANES), 1) == 0
+    low, high = pl.ds(0, LANES), pl.ds(LANES, HALF - LANES)
+    total_q[:, low] += jnp.where(edge, 0.5 * both[:, :LANES], both[:, :LANES])
+    total_q[:, high] += both[:, LANES:]
+    total_r[:, low] += jnp.where(edge, 0.25 * (ad[:, :LANES] - bc[:, :LANES]), cross[:, :LANES])
+    total_r[:, high] += cross[:, LANES:]
+
 
 def largest(total_q, total_r):
     def body(i, acc):
         rows = pl.ds(pl.multiple_of(i * 32, 32), 32)
-        return jnp.maximum(acc, total_q[rows, :] + jnp.abs(total_r[rows, :]))
+        return jnp.maximum(acc, total_q[rows, :] + 2.0 * jnp.abs(total_r[rows, :]))
 
     return jnp.max(lax.fori_loop(0, ROWS // 32, body, jnp.zeros((32, HALF), jnp.float32)))
 
@@ -506,6 +496,7 @@
             pltpu.VMEM((dets, 2, FOLD, WIDE), f32),
             pltpu.VMEM((slots, 2, FOLD, WIDE), f32),
             pltpu.VMEM((2, ROWS, COLS), bf16),
+            pltpu.VMEM((COLS // 256, RADIX, 2 * FOLD, 256), f32),
             pltpu.VMEM((slots, ROWS, HALF), f32),
             pltpu.VMEM((slots, ROWS, HALF), f32),
             pltpu.VMEM((slots, 8, LANES), f32),
@@ -514,12 +505,12 @@
             pltpu.VMEM(second.shape, bf16),
             dma((5 + units,)),
             pltpu.SemaphoreType.REGULAR((bits,)),
-            dma((units,)), dma((units,)),
-            dma((bits, units)), dma((bits, units)),
-            dma((bits, units)), dma((bits, units)),
-            dma((2, units)), dma((2, units)),
-            dma((slots, n)), dma((slots, n)),
-            dma((slots, max(1, groups - 1), n)), dma((slots, max(1, groups - 1), n)),
+            dma, dma((units,)),
+            dma, dma((bits, units)),
+            dma, dma((bits, units)),
+            dma, dma((2, units)),
+            dma, dma((slots, n)),
+            dma((max(1, groups - 1),)), dma((slots, max(1, groups - 1))),
         ],
         compiler_params=pltpu.CompilerParams(
             collective_id=0, has_side_effects=True, vmem_limit_bytes=56 * 1024 * 1024

time: 84.6 us -> 75.6 us (0.89)
  Pallas kernels: 81.9 us -> 72.9 us
    pallas_call x1, Pallas kernels: 81.9 us -> 72.9 us  [body(): pl.pallas_call(kernel, out_shape=jax.ShapeDtypeStruct((2 * slots,), f32),...]
where the time goes in v3:
time: 75.6 us; the launch traced here: 75.4 us
  Pallas kernels  72.9 us (96%)
  between operations  1.29 us (2%)
  local copies, waits for them, and re-layouts  1.26 us (2%)
    pallas_call x1, Pallas kernels, body(): pl.pallas_call(kernel, out_shape=jax.ShapeDtypeStruct((2 * slots,), f32),...  72.9 us

profile of v3, /device:TPU:0, one launch (start us, length us, event | category | flops | bytes accessed | tf_op | source)
XLA Modules:
  0.0 75.4 jit_solution(114741129085521705)
XLA Ops:
  1.3 72.9 %search.1 = f32[4]{0:T(128)} custom-call(s32[2,16]{1,0:T(2,128)} %bitcast.13, s32[1]{0:T(128)S(6)} %copy.13.owner, s32[32]{0:T(128)} %cutoffs.1, s32[3]{0:T(128)} %slides.1, bf16[12,1024,128]{2,1,0:T(8,128)(2,1)} %bitcast.11, bf16[32,256,128]{2,1,0:T(8,128)(2,1)} %bitcast.12, bf16[4,256,256]{2,1,0:T(8,128)(2,1)} %constant.6.clone.first_hbm, ...), custom_call_target="tpu_custom_call" | custom-call | tf_op jit(solution)/shard_map/search/pallas_call | solution.py:480
  74.1 1.3 %fusion = (f32[2]{0:T(128)}, f32[2]{0:T(128)}) fusion(f32[4]{0:T(128)} %search.1), kind=kLoop, calls=%fused_computation | loop fusion | bytes 32 | tf_op jit(solution)/shard_map/slice | solution.py:523

commit v4 on v3

--- a/solution.py
+++ b/solution.py
@@ -1,3 +1,5 @@
+import functools
+
 import jax
 import jax.numpy as jnp
 import numpy as np
@@ -22,9 +24,17 @@
 MESH = pl.DeviceIdType.MESH
 CUT = 2
 EARLY = 8
-SWAP_STEP = 4
+GAP = 1
+PREPARE = 1
+LATE_FROM = 2
+LATE_STEP = 4
+SWAP_STEP = 2
 CROSS_STEP = 5
 CROSS_FROM = 1
+
+
+def use_chain(width, depth):
+    return width == 2 and 2 <= depth <= 8
 
 
 def turn_table(left_ids, right_ids, period):
@@ -49,16 +59,19 @@
 
 
 def kernel(
-    lists, owner, cutoffs, slides, strain, bank_hbm, first_hbm, twiddle_hbm, second_hbm,
+    width, lists, owner, cutoffs, slides, strain, bank_hbm, first_hbm, twiddle_hbm, second_hbm,
     results,
-    cand, other, heap, full, bank, picked, arrived, flat, row_phase, col_phase,
+    cand, other, heap, line, full, bank, picked, arrived, flat, row_phase, col_phase,
     turned, masked, twisted, sections, total_q, total_r, squares, first, twiddle, second,
     local_sem, near_sem, core_send, core_recv, rs_send, rs_recv, ag_send, ag_recv,
-    part_send, part_recv, swap_send, swap_recv, cross_send, cross_recv,
+    line_send, line_recv, part_send, part_recv, swap_send, swap_recv, cross_send, cross_recv,
 ):
     n, groups = lax.axis_size("tpl"), lax.axis_size("grp")
     me, group = lax.axis_index("tpl"), lax.axis_index("grp")
     bits = n.bit_length() - 2
+    depth = n // 2 // width
+    chain = use_chain(width, depth)
+    stages = 2 * depth if chain else 2 * bits
     core, chip = me % 2, me // 2
     dets = strain.shape[0] // (2 * CUT)
     units = dets * CUT
@@ -178,20 +191,19 @@
         cand[u, where] = jnp.where(i_own, cand[u, where], other[u, where])
 
     greet(0)
-    for u in range(units):
+    for k in range(bits):
+        pl.semaphore_wait(near_sem.at[k], 1)
+        if k + 1 < bits:
+            greet(k + 1)
+
+    def open_unit(u):
         mine_copies[u].wait()
         core_copy(u).wait_recv()
         choice(u, away(0))
         rs_copy(u, 0).start()
         choice(u, kept(1))
-        if u < bits:
-            pl.semaphore_wait(near_sem.at[u], 1)
-            if u + 1 < bits:
-                greet(u + 1)
-    for u in range(units, bits):
-        pl.semaphore_wait(near_sem.at[u], 1)
-        if u + 1 < bits:
-            greet(u + 1)
+
+    open_unit(0)
     bank_copy.wait()
     apart = sorted(range(2, n), key=lambda i: (i & 2, -i))
     alone = sum(1 for i in apart if not i & 2)
@@ -214,21 +226,111 @@
 
     for q in range(early):
         swap_start(q)
+    for u in range(1, units):
+        open_unit(u)
     for copy in tables:
         copy.start()
-    make_phases(slides, row_phase, col_phase)
-    for slot in range(slots):
-        arrived[slot, me] = bank[lists[slot, me]]
-    total_q[...] = jnp.zeros_like(total_q)
-    total_r[...] = jnp.zeros_like(total_r)
-
     def merge(u, k, where, start, size):
         agree = own_chip // (1 << k) == chip // (1 << k)
         offset = half - (half >> k) + start - base[k + 1]
         return jnp.where(agree, cand[u, where], heap[u, rows(offset, size)])
 
+    piece = half // (width * depth)
+    z = chip // width
+    near = me % (2 * width)
+    onward = (jnp.minimum(z + 1, depth - 1) * 2 * width + near, jnp.maximum(z - 1, 0) * 2 * width + near)
+
+    def strip(j):
+        return rows(bit[0] * (half // 2) + j * piece, piece)
+
+    def pane(j):
+        return rows(j * piece, piece)
+
+    def line_copy(way, u, j, first=False):
+        src = cand.at[u, strip(j)] if first else line.at[way, u, pane(j)]
+        return remote(
+            src, line.at[way, u, pane(j)], line_send, line_recv.at[way, u, j], tpl=onward[way]
+        )
+
+    def spread_copy(way, u, j):
+        at = full.at[2 * u + core, strip(j)]
+        return remote(at, at, ag_send, ag_recv.at[u, j], tpl=onward[way])
+
+    def hand_copy(u, j):
+        at = full.at[2 * u + core, strip(j)]
+        return remote(at, at, rs_send, rs_recv.at[1, u], tpl=peers[0])
+
+    def chain_stage(u, e):
+        line_owns = own_chip // width == z
+        if e == 0:
+            rs_copy(u, 0).wait_recv()
+            cand[u, kept(1)] = merge(u, 0, kept(1), base[1], half // 2)
+        if e < depth - 1:
+            for way in range(2):
+                behind = z if way == 0 else depth - 1 - z
+                j = depth - 1 - e + z if way == 0 else e - (depth - 1 - z)
+
+                @pl.when(behind == 0)
+                def _():
+                    line_copy(way, u, depth - 1 - e if way == 0 else e, True).start()
+
+                if e > 0:
+                    @pl.when((behind > 0) & (behind <= e))
+                    def _():
+                        line_copy(way, u, j).wait_recv()
+                        line[way, u, pane(j)] = jnp.where(line_owns, cand[u, strip(j)], line[way, u, pane(j)])
+                        line_copy(way, u, j).start()
+        elif e == depth - 1:
+            value = cand[u, strip(z)]
+
+            @pl.when(z == 0)
+            def _():
+                line_copy(1, u, z).wait_recv()
+                full[2 * u + core, strip(z)] = jnp.where(line_owns, value, line[1, u, pane(z)])
+                spread_copy(0, u, z).start()
+
+            @pl.when(z == depth - 1)
+            def _():
+                line_copy(0, u, z).wait_recv()
+                full[2 * u + core, strip(z)] = jnp.where(line_owns, value, line[0, u, pane(z)])
+                spread_copy(1, u, z).start()
+
+            @pl.when((z > 0) & (z < depth - 1))
+            def _():
+                line_copy(0, u, z).wait_recv()
+                line_copy(1, u, z).wait_recv()
+                other_side = jnp.where(own_chip // width < z, line[0, u, pane(z)], line[1, u, pane(z)])
+                full[2 * u + core, strip(z)] = jnp.where(line_owns, value, other_side)
+                spread_copy(0, u, z).start()
+                spread_copy(1, u, z).start()
+
+            hand_copy(u, z).start()
+        elif e < 2 * depth - 1:
+            h = e - (depth - 1)
+            for way in range(2):
+                j = z - h if way == 0 else z + h
+                ahead = depth - 1 - z if way == 0 else z
+
+                @pl.when(z >= h if way == 0 else z + h < depth)
+                def _():
+                    spread_copy(way, u, j).wait_recv()
+
+                    @pl.when(ahead > 0)
+                    def _():
+                        spread_copy(way, u, j).start()
+
+                    hand_copy(u, j).start()
+            if h == depth - 1:
+                part_copy(u, core, 0).start()
+        else:
+            at = full.at[2 * u + core, away(0)]
+            remote(at, at, rs_send, rs_recv.at[1, u], tpl=peers[0]).wait_recv()
+            part_copy(u, core, 1).start()
+
     def stage(u, e):
-        if e < bits:
+        if chain:
+            chain_stage(u, e)
+        elif e < bits:
             k = e
             rs_copy(u, k).wait_recv()
             if k + 1 < bits:
@@ -248,11 +350,14 @@
             if k < 2:
                 part_copy(u, core, 1 - k).start()
 
-    talk = units + 2 * bits - 1
-    swap_step = max(SWAP_STEP, -(-(len(queue) - early) // (talk - 3)))
+    opening = [u + (GAP if chain and u // CUT == dets - 1 else 0) for u in range(units)]
+    talk = opening[-1] + stages
+    swap_step = SWAP_STEP if chain else max(SWAP_STEP, -(-(len(queue) - early) // (talk - 3)))
     cross_step = max(CROSS_STEP, -(-len(queue) // (talk - CROSS_FROM)))
-    swap_slots = [range(early + t * swap_step, min(len(queue), early + (t + 1) * swap_step)) for t in range(talk)]
-    ends = [min(len(queue), (t - CROSS_FROM + 1) * cross_step, early + max(0, t - 1) * swap_step) for t in range(talk)]
+    steps_of = [swap_step if t < LATE_FROM or not chain else LATE_STEP for t in range(talk)]
+    starts = [min(len(queue), early + sum(steps_of[:t])) for t in range(talk + 1)]
+    swap_slots = [range(starts[t], starts[t + 1]) for t in range(talk)]
+    ends = [min(len(queue), (t - CROSS_FROM + 1) * cross_step, starts[max(0, t - 1)]) for t in range(talk)]
     ends = [max(0, end) if t >= CROSS_FROM else 0 for t, end in enumerate(ends)] + [len(queue)]
     cross_slots = [range(ends[t - 1] if t else 0, ends[t]) for t in range(talk + 1)]
     swap_slots.append(())
@@ -260,13 +365,16 @@
     landed = [
         max(t for t in range(talk) if any(queue[q][0] == slot for q in cross_slots[t])) for slot in range(slots)
     ]
-    turn_at = [u + 2 * bits for u in range(units)]
+    turn_at = [at + stages for at in opening]
     mask_at = [at + 1 for at in landed]
     pairs = sorted(
         (max(turn_at[CUT * (d + 1) - 1], mask_at[slot]), d, slot) for d in range(dets) for slot in range(slots)
     )
     filter_at = [ready for ready, _, _ in pairs]
-    steps = max(filter_at[-1], units + 2 * bits, landed[-1]) + 1
+    if chain:
+        for f in range(1, len(pairs)):
+            filter_at[f] = max(filter_at[f], min(filter_at[f - 1] + 1, talk - 1))
+    steps = max(filter_at[-1], talk, landed[-1]) + 1
 
     def choose(t, pairs):
         value, hit = 0, False
@@ -278,13 +386,23 @@
         for at in range(talk):
             @pl.when(t == at)
             def _():
-                for e in range(2 * bits):
-                    if 0 <= at - e < units:
-                        stage(at - e, e)
+                for e in range(stages):
+                    if at - e in opening:
+                        stage(opening.index(at - e), e)
                 for q in cross_slots[at]:
                     cross_start(q)
                 for q in swap_slots[at]:
                     swap_start(q)
+
+        @pl.when(t == PREPARE)
+        def _():
+            make_phases(slides, row_phase, col_phase)
+            for slot in range(slots):
+                arrived[slot, me] = bank[lists[slot, me]]
+            total_q[...] = jnp.zeros_like(total_q)
+            total_r[...] = jnp.zeros_like(total_r)
+            for copy in tables:
+                copy.wait()
 
         u, now = choose(t, list(zip(turn_at, range(units))))
 
@@ -321,17 +439,29 @@
         at = full.at[2 * u + 1 - core, kept(1) if which == 0 else away(0)]
         return remote(at, at, part_send, part_recv.at[which, u], tpl=partner)
 
-    for copy in tables:
-        copy.wait()
     lax.fori_loop(0, steps, step_body, 0)
 
     def sent(at, semaphore):
         remote(at, at, semaphore, core_recv.at[0], tpl=partner).wait_send()
 
     walk = heap.at[:, pl.ds(0, half - (half >> bits))]
+    if chain:
+        sent(other, rs_send)
+        sent(other.at[:, pl.ds(0, (depth - 1) * piece)], line_send)
+        inner = (z > 0) & (z < depth - 1)
+
+        @pl.when(inner)
+        def _():
+            sent(other.at[:, pl.ds(0, (depth + 1) * piece)], ag_send)
+
+        @pl.when(jnp.logical_not(inner))
+        def _():
+            sent(other.at[:, pl.ds(0, piece)], ag_send)
+    else:
+        sent(walk, rs_send)
+        sent(walk, ag_send)
     for at, semaphore in (
-        (other, core_send), (walk, rs_send), (walk, ag_send), (other, part_send),
-        (picked.at[:, pl.ds(0, n - 1)], swap_send),
+        (other, core_send), (other, part_send), (picked.at[:, pl.ds(0, n - 1)], swap_send),
     ):
         sent(at, semaphore)
     for g in range(1, groups):
@@ -461,9 +591,11 @@
     return jnp.max(lax.fori_loop(0, ROWS // 32, body, jnp.zeros((32, HALF), jnp.float32)))
 
 
-def body(strain_slots, templates, cutoffs, lists, owner, slides):
+def body(width, strain_slots, templates, cutoffs, lists, owner, slides):
     n, groups = lax.axis_size("tpl"), lax.axis_size("grp")
     bits = n.bit_length() - 2
+    depth = n // 2 // width
+    chain = use_chain(width, depth)
     dets, bins = strain_slots.shape[1], strain_slots.shape[3]
     units, half = dets * CUT, bins // LANES // CUT
     strain = strain_slots[0].reshape(dets, 2, bins // LANES, LANES).transpose(0, 2, 1, 3)
@@ -478,7 +610,7 @@
     dma, bf16, f32 = pltpu.SemaphoreType.DMA, jnp.bfloat16, jnp.float32
     hrow = bank.shape[1] // groups
     results = pl.pallas_call(
-        kernel,
+        functools.partial(kernel, width),
         out_shape=jax.ShapeDtypeStruct((2 * slots,), f32),
         in_specs=[smem] * 4 + [hbm] * 5,
         out_specs=smem,
@@ -486,6 +618,7 @@
             pltpu.VMEM((units, half, LANES), bf16),
             pltpu.VMEM((units, half, LANES), bf16),
             pltpu.VMEM((units, half, LANES), bf16),
+            pltpu.VMEM((2, units, half // width, LANES) if chain else (8, LANES), bf16),
             pltpu.VMEM((2 * units, half, LANES), bf16),
             pltpu.VMEM(bank.shape, bf16),
             pltpu.VMEM((slots, n, hrow, LANES), bf16),
@@ -507,7 +640,8 @@
             pltpu.SemaphoreType.REGULAR((bits,)),
             dma, dma((units,)),
             dma, dma((bits, units)),
-            dma, dma((bits, units)),
+            dma, dma((units, depth) if chain else (bits, units)),
+            dma, dma((2, units, depth) if chain else (1,)),
             dma, dma((2, units)),
             dma, dma((slots, n)),
             dma((max(1, groups - 1),)), dma((slots, max(1, groups - 1))),
@@ -533,4 +667,6 @@
         P("grp"),
     )
     out_specs = (P(("grp", "tpl")), P(("grp", "tpl")))
-    return jax.shard_map(body, mesh=mesh, in_specs=in_specs, out_specs=out_specs, check_vma=False)
+    width = len({d.coords[1] for d in mesh.devices[0].flat})
+    body_of = functools.partial(body, width)
+    return jax.shard_map(body_of, mesh=mesh, in_specs=in_specs, out_specs=out_specs, check_vma=False)

time: 75.6 us -> 73.9 us (0.978)
  Pallas kernels: 72.9 us -> 71.1 us
    pallas_call x1, Pallas kernels: 72.9 us -> 71.1 us  [body(): pl.pallas_call(functools.partial(kernel, width), out_shape=jax.ShapeDtype...]
where the time goes in v4:
time: 73.9 us; the launch traced here: 73.7 us
  Pallas kernels  71.1 us (96%)
  between operations  1.29 us (2%)
  local copies, waits for them, and re-layouts  1.26 us (2%)
    pallas_call x1, Pallas kernels, body(): pl.pallas_call(functools.partial(kernel, width), out_shape=jax.ShapeDtype...  71.1 us

profile of v4, /device:TPU:0, one launch (start us, length us, event | category | flops | bytes accessed | tf_op | source)
XLA Modules:
  0.0 73.7 jit_solution(5027571920709624797)
XLA Ops:
  1.3 71.1 %search.1 = f32[4]{0:T(128)} custom-call(s32[2,16]{1,0:T(2,128)} %bitcast.13, s32[1]{0:T(128)S(6)} %copy.13.owner, s32[32]{0:T(128)} %cutoffs.1, s32[3]{0:T(128)} %slides.1, bf16[12,1024,128]{2,1,0:T(8,128)(2,1)} %bitcast.11, bf16[32,256,128]{2,1,0:T(8,128)(2,1)} %bitcast.12, bf16[4,256,256]{2,1,0:T(8,128)(2,1)} %constant.6.clone.first_hbm, ...), custom_call_target="tpu_custom_call" | custom-call | tf_op jit(solution)/shard_map/search/pallas_call | solution.py:612
  72.4 1.3 %fusion = (f32[2]{0:T(128)}, f32[2]{0:T(128)}) fusion(f32[4]{0:T(128)} %search.1), kind=kLoop, calls=%fused_computation | loop fusion | bytes 32 | tf_op jit(solution)/shard_map/slice | solution.py:657

commit v5 on v4

--- a/solution.py
+++ b/solution.py
@@ -16,7 +16,8 @@
 HALF = COLS // 2
 LANES = 128
 CHUNKS = WIDE // LANES
-TALL = 2 * FOLD * CHUNKS
+PITCH = 2 * CHUNKS + 8
+TALL = FOLD * PITCH
 
 two_pi = 6.283185307179586
 eps_norm = 1e-06
@@ -491,20 +492,24 @@
 
 
 def tile(flat, i, c, part):
-    return flat[pl.ds((i * 8 * CHUNKS + c) * 2 + part, 8, stride=2 * CHUNKS), :]
+    return flat[pl.ds(i * 8 * PITCH + c * 2 + part, 8, stride=PITCH), :]
 
 
 def turn_unit(source, flat, row_phase, col_phase, turned, d, q):
-    half, size = source.shape[1], 256
+    half = source.shape[1]
     high = FOLD // CUT
+
+    span = 2 * CHUNKS
 
     def widen(i, _):
         for h in range(2):
-            at = pl.ds(pl.multiple_of(i * size, size), size)
-            flat[pl.ds(pl.multiple_of(h * half + i * size, size), size), :] = source[h, at, :].astype(jnp.float32)
+            for r in range(8):
+                at = pl.ds(pl.multiple_of((i * 8 + r) * span, span), span)
+                to = pl.ds(pl.multiple_of((h * (half // span) + i * 8 + r) * PITCH, 8), span)
+                flat[to, :] = source[h, at, :].astype(jnp.float32)
         return 0
 
-    lax.fori_loop(0, half // size, widen, 0)
+    lax.fori_loop(0, half // (8 * span), widen, 0)
 
     def body(i, _):
         at = pl.ds(pl.multiple_of(q * high + i * 8, 8), 8)
@@ -525,7 +530,9 @@
     shards, shard = source.shape[0], source.shape[1]
 
     def body(i, _):
-        flat[pl.ds(pl.multiple_of(i * shard, shard), shard), :] = source[i].astype(jnp.float32)
+        for r in range(shard // (2 * CHUNKS)):
+            to = pl.ds(pl.multiple_of((i * (shard // (2 * CHUNKS)) + r) * PITCH, 8), 2 * CHUNKS)
+            flat[to, :] = source[i, r * 2 * CHUNKS : (r + 1) * 2 * CHUNKS, :].astype(jnp.float32)
         return 0
 
     lax.fori_loop(0, shards, body, 0)

time: 73.9 us -> 71.7 us (0.970)
  Pallas kernels: 71.1 us -> 68.7 us
    pallas_call x1, Pallas kernels: 71.1 us -> 68.7 us  [body(): pl.pallas_call(functools.partial(kernel, width), out_shape=jax.ShapeDtype...]
where the time goes in v5:
time: 71.7 us; the launch traced here: 71.2 us
  Pallas kernels  68.7 us (96%)
  between operations  1.29 us (2%)
  local copies, waits for them, and re-layouts  1.26 us (2%)
    pallas_call x1, Pallas kernels, body(): pl.pallas_call(functools.partial(kernel, width), out_shape=jax.ShapeDtype...  68.7 us

profile of v5, /device:TPU:0, one launch (start us, length us, event | category | flops | bytes accessed | tf_op | source)
XLA Modules:
  0.0 71.2 jit_solution(16470307984882872607)
XLA Ops:
  1.3 68.7 %search.1 = f32[4]{0:T(128)} custom-call(s32[2,16]{1,0:T(2,128)} %bitcast.13, s32[1]{0:T(128)S(6)} %copy.13.owner, s32[32]{0:T(128)} %cutoffs.1, s32[3]{0:T(128)} %slides.1, bf16[12,1024,128]{2,1,0:T(8,128)(2,1)} %bitcast.11, bf16[32,256,128]{2,1,0:T(8,128)(2,1)} %bitcast.12, bf16[4,256,256]{2,1,0:T(8,128)(2,1)} %constant.6.clone.first_hbm, ...), custom_call_target="tpu_custom_call" | custom-call | tf_op jit(solution)/shard_map/search/pallas_call | solution.py:619
  69.9 1.3 %fusion = (f32[2]{0:T(128)}, f32[2]{0:T(128)}) fusion(f32[4]{0:T(128)} %search.1), kind=kLoop, calls=%fused_computation | loop fusion | bytes 32 | tf_op jit(solution)/shard_map/slice | solution.py:664
